TPU v7x, 512 devices: a whole 4x8x8 slice. The times are simulated.
512 devices in a mesh: layer: 16 (over z, core), col: 32 (over x, y).
Axes of the slice: x: 4, y: 8, z: 8, core: 2. Of those that a mesh axis runs over, the one named last changes fastest.
Arguments:
- factors: bfloat16 [16, 32, 2048, 64], P('layer', 'col'), may hold values from -0.9 to 0.9
- cores: float32 [16, 64, 64], P('layer'), may hold values from -2 to 6, as said below
- tile_list: int32 [256, 2], P('col'), may hold values from 0 to 31, as said below
- probes: bfloat16 [2048, 256, 64], P(None, 'col'), may hold values from -6 to 6
Outputs:
- basis: float32 [2048, 256, 64], P('layer', 'col')
- update_right: float32 [2048, 256, 64], P('layer', 'col')
Inputs may be any that keep to these rules, and one draw needn't show every extreme that they name: `tile_list`: each row is a block row and a block column of a tile of the lower triangle: the first is not below the second. `cores`: each matrix is symmetric positive definite: a Gram matrix plus a positive diagonal.
All inputs are finite; a program needn't handle non-finite values.
Results may differ from a plain program's by a relative error of at most 0.02.
Values may be sent and summed in bfloat16 or wider, within the bound.
No kernel may reach another device: no remote copies, remote signals or barrier semaphores. Data moves between devices by JAX's collectives and lax.ppermute only.
A program may use at most 64 MiB of HBM per device.

v0:
```python
import math

import jax
import jax.numpy as jnp
from jax import lax
from jax.experimental import pallas as pl
from jax.experimental.pallas import tpu as pltpu
from jax.sharding import Mesh, PartitionSpec as P


F32 = jnp.float32
BF16 = jnp.bfloat16
HIGHEST = lax.Precision.HIGHEST

NZ = 8
NT = 8
RANK = 64
PANELS = 8
DEPTH = PANELS * RANK
ROWS = 256
HALF = 128
BUNDLES = 18
EXTRA = 16


def nt_dot(a, b, precision=None):
    return lax.dot_general(
        a, b, (((1,), (1,)), ((), ())), precision=precision, preferred_element_type=F32
    )


def nn_dot(a, b, precision=None):
    return lax.dot_general(
        a, b, (((1,), (0,)), ((), ())), precision=precision, preferred_element_type=F32
    )


def split3(x):
    hi = x.astype(BF16)
    rest = x - hi.astype(F32)
    mid = rest.astype(BF16)
    low = (rest - mid.astype(F32)).astype(BF16)
    return hi, mid, low


def slice_kernel(f_ref, cores_ref, o_ref, sem):
    copies = []
    for q in range(NZ):
        copies.append(
            pltpu.make_async_copy(
                f_ref.at[:, q * ROWS:(q + 1) * ROWS], o_ref.at[q, :, 0:ROWS], sem.at[q]
            )
        )
        copies[q].start()
    one, two, _ = split3(cores_ref[...])
    both = jnp.concatenate([one, two], axis=1)
    for q in range(NZ):
        o_ref[q, :, ROWS:ROWS + 2 * RANK] = both
    for copy in copies:
        copy.wait()


def in_hbm(x):
    return pltpu.with_memory_space_constraint(x, pltpu.HBM)


def either_kernel(side_ref, low_ref, high_ref, o_ref, sem):
    @pl.when(side_ref[0] == 0)
    def _():
        pltpu.make_async_copy(low_ref, o_ref, sem).start()

    @pl.when(side_ref[0] != 0)
    def _():
        pltpu.make_async_copy(high_ref, o_ref, sem).start()

    pltpu.make_async_copy(low_ref, o_ref, sem).wait()


def either(low, high):
    side = lax.axis_index("core").astype(jnp.int32).reshape(1)
    anywhere = pl.BlockSpec(memory_space=pl.ANY)
    return pl.pallas_call(
        either_kernel,
        out_shape=jax.ShapeDtypeStruct(low.shape, low.dtype),
        in_specs=[pl.BlockSpec(memory_space=pltpu.SMEM), anywhere, anywhere],
        out_specs=anywhere,
        scratch_shapes=[pltpu.SemaphoreType.DMA(())],
    )(side, low, high)


def spread(own):
    def send(value, x_step, y_step):
        pairs = []
        for x in range(4):
            for y in range(8):
                if x_step is not None:
                    pairs.append((x * 8 + y, (x + x_step) % 4 * 8 + y))
                pairs.append((32 + x * 8 + y, 32 + x * 8 + (y + y_step) % 8))
        return lax.ppermute(value, ("core", "x", "y"), pairs)

    def bundle_send(value, y_step, x_step):
        pairs = []
        for x in range(4):
            for y in range(8):
                pairs.append((x * 8 + y, x * 8 + (y + y_step) % 8))
                if x_step is not None:
                    pairs.append((32 + x * 8 + y, 32 + (x + x_step) % 4 * 8 + y))
        return lax.ppermute(value, ("core", "x", "y"), pairs)

    up1 = send(own, 1, 1)
    down1 = send(own, -1, -1)
    up2 = send(up1, 1, 1)
    down2 = send(down1, None, -1)
    up3 = send(up2, None, 1)
    down3 = send(down2, None, -1)
    up4 = send(up3, None, 1)
    near = [jnp.stack([own, up1]), jnp.stack([down1, up2])]
    far = [jnp.stack([down2, up3]), jnp.stack([down3, up4])]
    out1, out2, out3, out4, out5, out6 = ([None, None] for _ in range(6))
    for h in range(2):
        out1[h] = bundle_send(near[h], 1, 1)
        out2[h] = bundle_send(near[h], -1, -1)
    for h in range(2):
        out3[h] = bundle_send(out1[h], 1, 1)
        out4[h] = bundle_send(either(out2[h], far[h]), -1, -1)
    for h in range(2):
        out5[h] = bundle_send(either(out3[h], far[h]), 1, 1)
        out6[h] = bundle_send(out4[h], -1, -1)
    out7 = bundle_send(out3[0], 2, None)
    out8 = bundle_send(out4[1], -2, None)
    return (*near, *far, *out1, *out2, *out3, *out4, *out5, *out6, out7, out8)


def pick(index, *values):
    out = jnp.full_like(index, values[0])
    for number, value in enumerate(values[1:], 1):
        out = jnp.where(index == number, value, out)
    return out


def locate(rows):
    dx = (lax.axis_index("x").astype(jnp.int32) - rows // 8) % 4
    dy = (lax.axis_index("y").astype(jnp.int32) - rows % 8) % 8
    lower = lax.axis_index("core") == 0
    place0 = pick(dx, 0, 1, 3, 2)
    half0 = place0 // 2
    which0 = pick(dy, 0, 4, 8, 12, 16, 14, 10, 6) + half0
    place1 = pick(dy, 0, 1, 3, 1, 3, 2, 0, 2)
    half1 = place1 // 2
    which1 = jnp.where((dy <= 2) | (dy == 7), pick(dx, 0, 4, 8, 6), pick(dx, 2, 12, 14, 10)) + half1
    return jnp.where(lower, which0, which1), jnp.where(lower, place0 - 2 * half0, place1 - 2 * half1)


def sketch_kernel(first_ref, second_ref, z_ref, probe_ref, *refs):
    bundles, refs = refs[0:BUNDLES], refs[BUNDLES:]
    o_ref, left_ref, right_ref, slot_ref, sem_right, sem_left, sem_probe = refs
    start = pl.multiple_of(z_ref[0] * ROWS, ROWS)

    def fetch(place_ref, t, out_ref, sem):
        which, at = place_ref[0, t], place_ref[1, t]

        def choose(low, high):
            if high - low == 1:
                pltpu.make_async_copy(bundles[low].at[at], out_ref.at[t], sem.at[t]).start()
                return
            middle = (low + high) // 2

            @pl.when(which < middle)
            def _():
                choose(low, middle)

            @pl.when(which >= middle)
            def _():
                choose(middle, high)

        choose(0, BUNDLES)

    def arrived(t, out_ref, sem):
        pltpu.make_async_copy(bundles[0].at[0], out_ref.at[t], sem.at[t]).wait()

    probes = []
    for t in range(NT):
        probes.append(
            pltpu.make_async_copy(probe_ref.at[t, :, pl.ds(start, ROWS)], slot_ref.at[t], sem_probe.at[t])
        )
        probes[t].start()
        fetch(second_ref, t, right_ref, sem_right)
    for t in range(NT):
        fetch(first_ref, t, left_ref, sem_left)
    for t in range(NT):
        probes[t].wait()
        arrived(t, right_ref, sem_right)
        o_ref[t] = nt_dot(slot_ref[t], right_ref[t]).astype(BF16)
    for t in range(NT):
        arrived(t, left_ref, sem_left)


def core_products(total, cores_ref):
    parts = []
    for k in range(PANELS):
        block = total[:, k * RANK:(k + 1) * RANK]
        parts.append(nt_dot(block, cores_ref[k], HIGHEST))
    return parts


def first_kernel(part_ref, cores_ref, o_ref):
    total = part_ref[0].astype(F32)
    for q in range(1, NZ):
        total = total + part_ref[q].astype(F32)
    parts = core_products(total, cores_ref)
    for k in range(PANELS):
        half = parts[k].astype(BF16)
        for q in range(NZ):
            o_ref[q, :, k * RANK:(k + 1) * RANK] = half


def sample_kernel(core_ref, f_ref, o_ref):
    for t in range(NT):
        o_ref[t] = nn_dot(core_ref[t], f_ref[t]).astype(BF16)


def pack_gram(gram):
    row = lax.broadcasted_iota(jnp.int32, (RANK, RANK), 0)
    col = lax.broadcasted_iota(jnp.int32, (RANK, RANK), 1)
    one, two, three = (part.astype(F32) for part in split3(gram))
    diag = jnp.sum(jnp.where(row == col, two, 0.0), axis=1, keepdims=True)
    last = jnp.sum(jnp.where((row == RANK - 1) & (col == RANK - 1), two, 0.0), axis=(0, 1), keepdims=True)
    upper = jnp.where(col == row + 1, diag, 0.0)
    upper = jnp.where((row == 0) & (col == RANK - 1), last, upper)
    return jnp.where(col <= row, one, jnp.transpose(two)), jnp.where(col <= row, three, upper)


def unpack_gram(left, right):
    row = lax.broadcasted_iota(jnp.int32, (RANK, RANK), 0)
    col = lax.broadcasted_iota(jnp.int32, (RANK, RANK), 1)
    corner = (row == 0) & (col == RANK - 1)
    last = jnp.sum(jnp.where(corner, right, 0.0), axis=(0, 1), keepdims=True)
    diag = jnp.sum(jnp.where(col == row + 1, right, 0.0), axis=1, keepdims=True)
    two_diag = jnp.where((row == col) & (row < RANK - 1), diag, 0.0)
    two_diag = jnp.where((row == RANK - 1) & (col == RANK - 1), last, two_diag)
    lower = col <= row
    one = jnp.where(lower, left, 0.0)
    three = jnp.where(lower, right, 0.0)
    two = jnp.where(col > row, left, 0.0)
    strict = jnp.where(col < row, one, 0.0) + jnp.where(col < row, three, 0.0)
    full_diag = jnp.where(row == col, one + (three + two_diag), 0.0)
    below = strict + jnp.where(col < row, jnp.transpose(two), 0.0)
    return below + full_diag + jnp.transpose(below)


def fold(x):
    return jnp.concatenate([x[EXTRA * b:EXTRA * (b + 1)] for b in range(4)], axis=1)


def unfold(x):
    return jnp.concatenate([x[:, 128 * b:128 * (b + 1)] for b in range(4)], axis=0)


def gram_kernel(own_ref, other_ref, f_ref, o_ref):
    for t in range(NT):
        total = own_ref[t].astype(F32) + other_ref[t].astype(F32)
        gram = nt_dot(total, total, HIGHEST)
        hi = total.astype(BF16)
        low = (total - hi.astype(F32)).astype(BF16)
        both = nt_dot(jnp.concatenate([hi, low], axis=0), f_ref[t])
        o_ref[t, 0:RANK] = (both[0:RANK] + both[RANK:2 * RANK]).astype(BF16)
        left, right = pack_gram(gram)
        o_ref[t, RANK:RANK + EXTRA] = fold(jnp.concatenate([left, right], axis=1).astype(BF16))


def inverse_factor(gram):
    row_id = lax.broadcasted_iota(jnp.int32, (RANK, RANK), 0)
    col_id = lax.broadcasted_iota(jnp.int32, (RANK, RANK), 1)
    unit = jnp.where(row_id == col_id, 1.0, 0.0).astype(F32)
    work = jnp.concatenate([gram, unit], axis=1)
    blocks = [work[8 * b:8 * b + 8, :] for b in range(RANK // 8)]
    sub = lax.broadcasted_iota(jnp.int32, (8, 2 * RANK), 0)
    for p in range(RANK):
        home, at = divmod(p, 8)
        row = blocks[home][at:at + 1, :]
        pivot = row[:, p:p + 1]
        scaled = row * (1.0 / pivot)
        for b in range(home, RANK // 8):
            col = jnp.broadcast_to(blocks[b][:, p:p + 1], (8, 2 * RANK))
            if b == home:
                col = jnp.where(sub > at, col, 0.0)
            blocks[b] = blocks[b] - col * scaled
    work = jnp.concatenate(blocks, axis=0)
    diag = jnp.sum(jnp.where(row_id == col_id, work[:, 0:RANK], 0.0), axis=1, keepdims=True)
    return work[:, RANK:2 * RANK] * (1.0 / jnp.sqrt(diag))


def second_kernel(part_ref, cores_ref, o_ref):
    summed = part_ref[0].astype(F32)
    for q in range(1, NZ):
        summed = summed + part_ref[q].astype(F32)
    total = summed[0:RANK]
    packed = unfold(summed[RANK:RANK + EXTRA])
    gram = unpack_gram(packed[:, 0:RANK], packed[:, RANK:2 * RANK])
    inverse = inverse_factor(gram)
    projected = nn_dot(inverse, total, HIGHEST)
    parts = core_products(projected, cores_ref)
    one, two, _ = split3(inverse)
    extra = fold(jnp.concatenate([one, two], axis=1))
    for q in range(NZ):
        for k in range(PANELS):
            o_ref[q, 0:RANK, k * RANK:(k + 1) * RANK] = parts[k].astype(BF16)
        o_ref[q, RANK:RANK + EXTRA] = extra


def final_kernel(side_ref, core_ref, own_ref, other_ref, f_ref, basis_ref, keep_ref, send_ref):
    upper = side_ref[0] == 1
    for t in range(NT):
        extra = unfold(core_ref[t, RANK:RANK + EXTRA]).astype(F32)
        inverse = extra[:, 0:RANK] + extra[:, RANK:2 * RANK]
        total = own_ref[t].astype(F32) + other_ref[t].astype(F32)
        half = jnp.where(upper, total[:, HALF:ROWS], total[:, 0:HALF])
        basis_ref[t] = nn_dot(inverse, half, HIGHEST) * math.sqrt(2048.0)
        part = nn_dot(core_ref[t, 0:RANK], f_ref[t])
        first, last = part[:, 0:HALF], part[:, HALF:ROWS]
        keep_ref[t] = jnp.where(upper, last, first)
        send_ref[t] = jnp.where(upper, first, last).astype(BF16)


def local(factors, cores, tile_list, probes):
    swap = [(0, 1), (1, 0)]
    z = lax.axis_index("z").astype(jnp.int32).reshape(1)
    side = lax.axis_index("core").astype(jnp.int32).reshape(1)
    row_first = tile_list[:, 0].astype(jnp.int32)
    row_second = tile_list[:, 1].astype(jnp.int32)
    params = pltpu.CompilerParams(vmem_limit_bytes=32 * 1024 * 1024)

    smem = pl.BlockSpec(memory_space=pltpu.SMEM)
    hbm = pl.BlockSpec(memory_space=pl.ANY)
    vmem = pl.BlockSpec(memory_space=pltpu.VMEM)

    def call(kernel, out_shape, in_specs, *args, scratch=()):
        return pl.pallas_call(
            kernel,
            out_shape=out_shape,
            in_specs=in_specs,
            out_specs=jax.tree.map(lambda _: vmem, out_shape),
            scratch_shapes=scratch,
            compiler_params=params,
        )(*args)

    def shape(*dims, dtype=BF16):
        return jax.ShapeDtypeStruct(dims, dtype)

    def exchange(x):
        return lax.all_to_all(x, "z", 0, 0, tiled=True)

    mine = jnp.transpose(factors[0, 0], (1, 0))
    sliced = call(
        slice_kernel,
        shape(NZ, RANK, ROWS + 2 * RANK),
        [hbm, vmem],
        in_hbm(mine),
        cores[0],
        scratch=[pltpu.SemaphoreType.DMA((NZ,))],
    )
    panels = exchange(sliced)
    pieces = panels[:, :, ROWS:ROWS + 2 * RANK].astype(F32)
    all_cores = pieces[:, :, 0:RANK] + pieces[:, :, RANK:2 * RANK]
    bundles = spread(panels[:, :, 0:ROWS].reshape(DEPTH, ROWS))
    probe = in_hbm(jnp.transpose(probes, (1, 2, 0)))
    block = shape(NT, DEPTH, ROWS)
    sketch, left, right = call(
        sketch_kernel,
        (shape(NT, RANK, DEPTH), block, block),
        [smem, smem, smem] + [hbm] * (1 + BUNDLES),
        jnp.stack(locate(row_first)),
        jnp.stack(locate(row_second)),
        z,
        probe,
        *(in_hbm(bundle) for bundle in bundles),
        scratch=[pltpu.VMEM((NT, RANK, ROWS), BF16)] + [pltpu.SemaphoreType.DMA((NT,))] * 3,
    )
    first = call(first_kernel, shape(NZ, RANK, DEPTH), [vmem] * 2, exchange(sketch), all_cores)
    own = call(sample_kernel, shape(NT, RANK, ROWS), [vmem] * 2, exchange(first), left)
    other = lax.ppermute(own, "core", swap)
    tall = (NT, RANK + EXTRA, DEPTH)
    stacked = call(gram_kernel, shape(*tall), [vmem] * 3, own, other, left)
    second = call(second_kernel, shape(*tall), [vmem] * 2, exchange(stacked), all_cores)
    half = (NT, RANK, HALF)
    basis, keep, send = call(
        final_kernel,
        (shape(*half, dtype=F32), shape(*half, dtype=F32), shape(*half)),
        [smem] + [vmem] * 4,
        side,
        exchange(second),
        own,
        other,
        right,
    )
    update = keep + lax.ppermute(send, "core", swap).astype(F32)
    return jnp.transpose(basis, (2, 0, 1)), jnp.transpose(update, (2, 0, 1))


def solution(mesh):
    fine = Mesh(mesh.devices.reshape(8, 2, 4, 8), ("z", "core", "x", "y"))
    layer, col = ("z", "core"), ("x", "y")
    placed = (
        P(layer, col, None, None),
        P(layer, None, None),
        P(col, None),
        P(None, col, None),
    )
    return jax.shard_map(
        local,
        mesh=fine,
        in_specs=placed,
        out_specs=(P(layer, col, None), P(layer, col, None)),
        check_vma=False,
    )
```

profile of v0, /device:TPU:1, one launch (start us, length us, event | category | flops | bytes accessed | tf_op | source)
XLA Modules:
  0.0 292.5 jit_solution(5228100244040347151)
XLA Ops:
  1.4 0.9 shard_map.59
  2.3 24.2 %all_to_all.25 = bf16[8,64,384]{2,1,0:T(8,128)(2,1)S(1)} all-to-all(bf16[8,64,384]{2,1,0:T(8,128)(2,1)S(1)} %shard_map.59), channel_id=1, replica_groups=mesh['z'=8,'core'=2,'x'=4,'y'=8] {'z'}, dimensions={0} | all-to-all | bytes 786432 | tf_op jit(solution)/shard_map/all_to_all | solution.py:351
  26.6 3.2 %collective-permute-start = (bf16[512,256]{1,0:T(8,128)(2,1)S(1)}, bf16[512,256]{1,0:T(8,128)(2,1)S(1)}, u32[]{:S(2)}, u32[]{:S(2)}) collective-permute-start(bf16[512,256]{1,0:T(8,128)(2,1)S(1)} %bitcast.57), channel_id=1, source_target_pairs={{0,8},{32,33},{1,9},{33,34},{2,10},{34,35},{3,11},{35,36},{4,12},{... | collective-permute-start | bytes 786440 | tf_op jit(solution)/shard_map/ppermute | solution.py:99
  29.8 3.8 %collective-permute-start.1 = (bf16[512,256]{1,0:T(8,128)(2,1)S(1)}, bf16[512,256]{1,0:T(8,128)(2,1)S(1)}, u32[]{:S(2)}, u32[]{:S(2)}) collective-permute-start(bf16[512,256]{1,0:T(8,128)(2,1)S(1)} %bitcast.58), channel_id=1, source_target_pairs={{0,24},{32,39},{1,25},{33,32},{2,26},{34,33},{3,27},{35,34},{4,28}... | collective-permute-start | bytes 786440 | tf_op jit(solution)/shard_map/ppermute | solution.py:99
  33.6 2.1 collective-permute-done
  35.7 1.9 collective-permute-start.2
  37.7 4.1 %collective-permute-start.9 = (bf16[2,512,256]{2,1,0:T(8,128)(2,1)S(1)}, bf16[2,512,256]{2,1,0:T(8,128)(2,1)S(1)}, u32[]{:S(2)}, u32[]{:S(2)}) collective-permute-start(bf16[2,512,256]{2,1,0:T(8,128)(2,1)S(1)} %pad_maximum_fusion.refs_0_), channel_id=1, source_target_pairs={{0,7},{32,56},{1,0},{33,57},{2,1},{34,58},{3,2},{35,59},{4,3},{36,... | collective-permute-start | bytes 1572872 | tf_op jit(solution)/shard_map/ppermute | solution.py:108
  41.8 4.6 %collective-permute-start.3 = (bf16[512,256]{1,0:T(8,128)(2,1)S(1)}, bf16[512,256]{1,0:T(8,128)(2,1)}, u32[]{:S(2)}, u32[]{:S(2)}) collective-permute-start(bf16[512,256]{1,0:T(8,128)(2,1)S(1)} %collective-permute-done.1), channel_id=1, source_target_pairs={{32,39},{33,32},{34,33},{35,34},{36,35},{37,36},{38,37},{39,38},{4... | collective-permute-start | bytes 786440 | tf_op jit(solution)/shard_map/ppermute | solution.py:99
  46.4 1.9 collective-permute-start.4
  48.4 1.9 collective-permute-start.7
  50.4 2.2 collective-permute-done.3
  52.5 5.3 %collective-permute-start.5 = (bf16[512,256]{1,0:T(8,128)(2,1)}, bf16[512,256]{1,0:T(8,128)(2,1)}, u32[]{:S(2)}, u32[]{:S(2)}) collective-permute-start(bf16[512,256]{1,0:T(8,128)(2,1)} %collective-permute-done.3), channel_id=1, source_target_pairs={{32,39},{33,32},{34,33},{35,34},{36,35},{37,36},{38,37},{39,38},{4... | collective-permute-start | bytes 786440 | tf_op jit(solution)/shard_map/ppermute | solution.py:99
  57.8 1.9 collective-permute-start.10
  59.8 3.4 %collective-permute-start.8 = (bf16[2,512,256]{2,1,0:T(8,128)(2,1)S(1)}, bf16[2,512,256]{2,1,0:T(8,128)(2,1)S(1)}, u32[]{:S(2)}, u32[]{:S(2)}) collective-permute-start(bf16[2,512,256]{2,1,0:T(8,128)(2,1)S(1)} %pad_maximum_fusion.1.refs_1_), channel_id=1, source_target_pairs={{0,1},{32,40},{1,2},{33,41},{2,3},{34,42},{3,4},{35,43},{4,5},{36,... | collective-permute-start | bytes 1572872 | tf_op jit(solution)/shard_map/ppermute | solution.py:108
  63.1 1.9 pad_maximum_fusion.2.high_ref.refs_2_
  65.8 17.0 %shard_map.60 = bf16[2,512,256]{2,1,0:T(8,128)(2,1)} custom-call(s32[1]{0:T(128)} %bitcast.side_ref, bf16[2,512,256]{2,1,0:T(8,128)(2,1)} %copy-done.4, bf16[2,512,256]{2,1,0:T(8,128)(2,1)} %pad_maximum_fusion.2.high_ref.refs_2_), custom_call_target="tpu_custom_call" | custom-call | tf_op jit(solution)/shard_map/pallas_call | solution.py:82
  82.8 3.1 %collective-permute-start.13 = (bf16[2,512,256]{2,1,0:T(8,128)(2,1)}, bf16[2,512,256]{2,1,0:T(8,128)(2,1)}, u32[]{:S(2)}, u32[]{:S(2)}) collective-permute-start(bf16[2,512,256]{2,1,0:T(8,128)(2,1)} %shard_map.60), channel_id=1, source_target_pairs={{0,7},{32,56},{1,0},{33,57},{2,1},{34,58},{3,2},{35,59},{4,3},{36,... | collective-permute-start | bytes 1572872 | tf_op jit(solution)/shard_map/ppermute | solution.py:108
  86.0 1.9 collective-permute-start.6
  87.9 2.2 collective-permute-start.11
  90.1 7.5 %collective-permute-done.6 = bf16[512,256]{1,0:T(8,128)(2,1)S(1)} collective-permute-done((bf16[512,256]{1,0:T(8,128)(2,1)}, bf16[512,256]{1,0:T(8,128)(2,1)S(1)}, u32[]{:S(2)}, u32[]{:S(2)}) %collective-permute-start.6) | collective-permute-done | bytes 262176 | tf_op jit(solution)/shard_map/ppermute | solution.py:99
  97.6 1.8 pad_maximum_fusion.3.high_ref.refs_3_
  99.4 2.2 collective-permute-start.12
  102.4 17.0 %shard_map.61 = bf16[2,512,256]{2,1,0:T(8,128)(2,1)} custom-call(s32[1]{0:T(128)} %bitcast.side_ref, bf16[2,512,256]{2,1,0:T(8,128)(2,1)} %copy-done.6, bf16[2,512,256]{2,1,0:T(8,128)(2,1)} %pad_maximum_fusion.3.high_ref.refs_3_), custom_call_target="tpu_custom_call" | custom-call | tf_op jit(solution)/shard_map/pallas_call | solution.py:82
  119.4 4.3 %collective-permute-start.14 = (bf16[2,512,256]{2,1,0:T(8,128)(2,1)}, bf16[2,512,256]{2,1,0:T(8,128)(2,1)S(1)}, u32[]{:S(2)}, u32[]{:S(2)}) collective-permute-start(bf16[2,512,256]{2,1,0:T(8,128)(2,1)} %shard_map.61), channel_id=1, source_target_pairs={{0,7},{32,56},{1,0},{33,57},{2,1},{34,58},{3,2},{35,59},{4,3},{36,... | collective-permute-start | bytes 1572872 | tf_op jit(solution)/shard_map/ppermute | solution.py:108
  123.7 1.9 collective-permute-start.17
  126.2 0.8 copy-done.7
  127.1 17.0 %shard_map.62 = bf16[2,512,256]{2,1,0:T(8,128)(2,1)} custom-call(s32[1]{0:T(128)} %bitcast.side_ref, bf16[2,512,256]{2,1,0:T(8,128)(2,1)} %copy-done.7, bf16[2,512,256]{2,1,0:T(8,128)(2,1)} %pad_maximum_fusion.2.high_ref.refs_2_), custom_call_target="tpu_custom_call" | custom-call | tf_op jit(solution)/shard_map/pallas_call | solution.py:82
  144.1 3.4 %collective-permute-start.15 = (bf16[2,512,256]{2,1,0:T(8,128)(2,1)}, bf16[2,512,256]{2,1,0:T(8,128)(2,1)S(1)}, u32[]{:S(2)}, u32[]{:S(2)}) collective-permute-start(bf16[2,512,256]{2,1,0:T(8,128)(2,1)} %shard_map.62), channel_id=1, source_target_pairs={{0,1},{32,40},{1,2},{33,41},{2,3},{34,42},{3,4},{35,43},{4,5},{36,... | collective-permute-start | bytes 1572872 | tf_op jit(solution)/shard_map/ppermute | solution.py:108
  148.2 0.8 copy-done.8
  149.0 17.0 %shard_map.63 = bf16[2,512,256]{2,1,0:T(8,128)(2,1)} custom-call(s32[1]{0:T(128)} %bitcast.side_ref, bf16[2,512,256]{2,1,0:T(8,128)(2,1)} %copy-done.8, bf16[2,512,256]{2,1,0:T(8,128)(2,1)} %pad_maximum_fusion.3.high_ref.refs_3_), custom_call_target="tpu_custom_call" | custom-call | tf_op jit(solution)/shard_map/pallas_call | solution.py:82
  166.0 1.9 collective-permute-start.16
  167.9 1.5 collective-permute-start.20
  169.4 4.6 %collective-permute-start.18 = (bf16[2,512,256]{2,1,0:T(8,128)(2,1)S(1)}, bf16[2,512,256]{2,1,0:T(8,128)(2,1)}, u32[]{:S(2)}, u32[]{:S(2)}) collective-permute-start(bf16[2,512,256]{2,1,0:T(8,128)(2,1)S(1)} %collective-permute-done.14.refs_11_), channel_id=1, source_target_pairs={{0,7},{32,56},{1,0},{33,57},{2,1},{34,58},{3,2},{35,59},{4,3},{36,... | collective-permute-start | bytes 1572872 | tf_op jit(solution)/shard_map/ppermute | solution.py:108
  176.5 3.6 %collective-permute-done.18.refs_15_ = bf16[2,512,256]{2,1,0:T(8,128)(2,1)} collective-permute-done((bf16[2,512,256]{2,1,0:T(8,128)(2,1)S(1)}, bf16[2,512,256]{2,1,0:T(8,128)(2,1)}, u32[]{:S(2)}, u32[]{:S(2)}) %collective-permute-start.18) | collective-permute-done | bytes 524320 | tf_op jit(solution)/shard_map/ppermute | solution.py:108
  180.9 5.3 %shard_map.64 = (bf16[8,64,512]{2,1,0:T(8,128)(2,1)}, bf16[8,512,256]{2,1,0:T(8,128)(2,1)S(1)}, bf16[8,512,256]{2,1,0:T(8,128)(2,1)S(1)}) custom-call(s32[2,8]{1,0:T(2,128)S(1)} %pad_add_fusion.first_ref, s32[2,8]{1,0:T(2,128)S(1)} %pad_add_fusion.1.second_ref, s32[1]{0:T(128)} %bitcast.3.z_ref, bf16[8,64,2048]{2,1,0:T(8,128)(2,1)} %bitcast.56, ...), custom_call_target="tpu_custom_call" | custom-call | tf_op jit(solution)/shard_map/pallas_call | solution.py:338
  186.2 1.3 copy-done
  187.5 3.5 %all-to-all-start.1 = ((bf16[8,64,512]{2,1,0:T(8,128)(2,1)}), bf16[8,64,512]{2,1,0:T(8,128)(2,1)S(1)}, u32[]{:S(2)}, u32[]{:S(2)}) async-start(bf16[8,64,512]{2,1,0:T(8,128)(2,1)} %get-tuple-element.8), calls=%async_computation.1 | async-start | bytes 1048576 | tf_op jit(solution)/shard_map/all_to_all | solution.py:351
  191.2 11.9 %all-to-all-done.1.part_ref = bf16[8,64,512]{2,1,0:T(8,128)(2,1)S(1)} async-done(((bf16[8,64,512]{2,1,0:T(8,128)(2,1)}), bf16[8,64,512]{2,1,0:T(8,128)(2,1)S(1)}, u32[]{:S(2)}, u32[]{:S(2)}) %all-to-all-start.1) | async-done | bytes 524320 | tf_op jit(solution)/shard_map/all_to_all | solution.py:351
  203.8 14.5 %all_to_all.26.core_ref = bf16[8,64,512]{2,1,0:T(8,128)(2,1)S(1)} all-to-all(bf16[8,64,512]{2,1,0:T(8,128)(2,1)S(1)} %shard_map.65), channel_id=1, replica_groups=mesh['z'=8,'core'=2,'x'=4,'y'=8] {'z'}, dimensions={0} | all-to-all | bytes 1048576 | tf_op jit(solution)/shard_map/all_to_all | solution.py:351
  218.8 12.6 %collective-permute-start.21 = (bf16[8,64,256]{2,1,0:T(8,128)(2,1)S(1)}, bf16[8,64,256]{2,1,0:T(8,128)(2,1)S(1)}, u32[]{:S(2)}, u32[]{:S(2)}) collective-permute-start(bf16[8,64,256]{2,1,0:T(8,128)(2,1)S(1)} %shard_map.66.own_ref), channel_id=1, source_target_pairs={{0,32},{32,0},{1,33},{33,1},{2,34},{34,2},{3,35},{35,3},{4,36},{36... | collective-permute-start | bytes 786440 | tf_op jit(solution)/shard_map/ppermute | solution.py:381
  231.5 1.1 collective-permute-done.21.other_ref
  232.6 1.4 shard_map.67
  234.0 23.3 %all_to_all.27.part_ref = bf16[8,80,512]{2,1,0:T(8,128)(2,1)S(1)} all-to-all(bf16[8,80,512]{2,1,0:T(8,128)(2,1)S(1)} %shard_map.67), channel_id=1, replica_groups=mesh['z'=8,'core'=2,'x'=4,'y'=8] {'z'}, dimensions={0} | all-to-all | bytes 1310720 | tf_op jit(solution)/shard_map/all_to_all | solution.py:351
  257.3 6.6 %shard_map.68 = bf16[8,80,512]{2,1,0:T(8,128)(2,1)S(1)} custom-call(bf16[8,80,512]{2,1,0:T(8,128)(2,1)S(1)} %all_to_all.27.part_ref, f32[8,64,64]{2,1,0:T(8,128)S(1)} %slice_add_fusion.cores_ref), custom_call_target="tpu_custom_call" | custom-call | tf_op jit(solution)/shard_map/pallas_call | solution.py:338
  263.9 22.3 %all_to_all.28.core_ref = bf16[8,80,512]{2,1,0:T(8,128)(2,1)S(1)} all-to-all(bf16[8,80,512]{2,1,0:T(8,128)(2,1)S(1)} %shard_map.68), channel_id=1, replica_groups=mesh['z'=8,'core'=2,'x'=4,'y'=8] {'z'}, dimensions={0} | all-to-all | bytes 1310720 | tf_op jit(solution)/shard_map/all_to_all | solution.py:351
  286.2 1.4 shard_map.69
  287.6 3.3 %collective-permute-start.22 = (bf16[8,64,128]{2,1,0:T(8,128)(2,1)S(1)}, bf16[8,64,128]{2,1,0:T(8,128)(2,1)S(1)}, u32[]{:S(2)}, u32[]{:S(2)}) collective-permute-start(bf16[8,64,128]{2,1,0:T(8,128)(2,1)S(1)} %get-tuple-element.13), channel_id=1, source_target_pairs={{0,32},{32,0},{1,33},{33,1},{2,34},{34,2},{3,35},{35,3},{4,36},{36... | collective-permute-start | bytes 393224 | tf_op jit(solution)/shard_map/ppermute | solution.py:396
  290.8 1.0 collective-permute-done.22
  (62 shorter events, 9.1 us)
Async XLA Ops:
  0.6 0.8 copy-start.2
  26.6 9.1 %collective-permute-start = (bf16[512,256]{1,0:T(8,128)(2,1)S(1)}, bf16[512,256]{1,0:T(8,128)(2,1)S(1)}, u32[]{:S(2)}, u32[]{:S(2)}) collective-permute-start(bf16[512,256]{1,0:T(8,128)(2,1)S(1)} %bitcast.57), channel_id=1, source_target_pairs={{0,8},{32,33},{1,9},{33,34},{2,10},{34,35},{3,11},{35,36},{4,12},{... | collective-permute-start | bytes 786440 | tf_op jit(solution)/shard_map/ppermute | solution.py:99
  29.8 12.0 %collective-permute-start.1 = (bf16[512,256]{1,0:T(8,128)(2,1)S(1)}, bf16[512,256]{1,0:T(8,128)(2,1)S(1)}, u32[]{:S(2)}, u32[]{:S(2)}) collective-permute-start(bf16[512,256]{1,0:T(8,128)(2,1)S(1)} %bitcast.58), channel_id=1, source_target_pairs={{0,24},{32,39},{1,25},{33,32},{2,26},{34,33},{3,27},{35,34},{4,28}... | collective-permute-start | bytes 786440 | tf_op jit(solution)/shard_map/ppermute | solution.py:99
  35.7 10.7 %collective-permute-start.2 = (bf16[512,256]{1,0:T(8,128)(2,1)S(1)}, bf16[512,256]{1,0:T(8,128)(2,1)S(1)}, u32[]{:S(2)}, u32[]{:S(2)}) collective-permute-start(bf16[512,256]{1,0:T(8,128)(2,1)S(1)} %collective-permute-done), channel_id=1, source_target_pairs={{0,8},{32,33},{1,9},{33,34},{2,10},{34,35},{3,11},{35,36},{4,12},{... | collective-permute-start | bytes 786440 | tf_op jit(solution)/shard_map/ppermute | solution.py:99
  37.7 61.7 %copy-start.3 = (bf16[2,512,256]{2,1,0:T(8,128)(2,1)}, bf16[2,512,256]{2,1,0:T(8,128)(2,1)S(1)}, u32[]{:S(2)}) copy-start(bf16[2,512,256]{2,1,0:T(8,128)(2,1)S(1)} %pad_maximum_fusion.refs_0_) | copy-start | bytes 1572868
  37.7 27.3 %collective-permute-start.9 = (bf16[2,512,256]{2,1,0:T(8,128)(2,1)S(1)}, bf16[2,512,256]{2,1,0:T(8,128)(2,1)S(1)}, u32[]{:S(2)}, u32[]{:S(2)}) collective-permute-start(bf16[2,512,256]{2,1,0:T(8,128)(2,1)S(1)} %pad_maximum_fusion.refs_0_), channel_id=1, source_target_pairs={{0,7},{32,56},{1,0},{33,57},{2,1},{34,58},{3,2},{35,59},{4,3},{36,... | collective-permute-start | bytes 1572872 | tf_op jit(solution)/shard_map/ppermute | solution.py:108
  41.8 10.7 %collective-permute-start.3 = (bf16[512,256]{1,0:T(8,128)(2,1)S(1)}, bf16[512,256]{1,0:T(8,128)(2,1)}, u32[]{:S(2)}, u32[]{:S(2)}) collective-permute-start(bf16[512,256]{1,0:T(8,128)(2,1)S(1)} %collective-permute-done.1), channel_id=1, source_target_pairs={{32,39},{33,32},{34,33},{35,34},{36,35},{37,36},{38,37},{39,38},{4... | collective-permute-start | bytes 786440 | tf_op jit(solution)/shard_map/ppermute | solution.py:99
  46.4 13.3 %collective-permute-start.4 = (bf16[512,256]{1,0:T(8,128)(2,1)S(1)}, bf16[512,256]{1,0:T(8,128)(2,1)}, u32[]{:S(2)}, u32[]{:S(2)}) collective-permute-start(bf16[512,256]{1,0:T(8,128)(2,1)S(1)} %collective-permute-done.2), channel_id=1, source_target_pairs={{32,33},{33,34},{34,35},{35,36},{36,37},{37,38},{38,39},{39,32},{4... | collective-permute-start | bytes 786440 | tf_op jit(solution)/shard_map/ppermute | solution.py:99
  48.4 39.5 %collective-permute-start.7 = (bf16[2,512,256]{2,1,0:T(8,128)(2,1)S(1)}, bf16[2,512,256]{2,1,0:T(8,128)(2,1)S(1)}, u32[]{:S(2)}, u32[]{:S(2)}) collective-permute-start(bf16[2,512,256]{2,1,0:T(8,128)(2,1)S(1)} %pad_maximum_fusion.refs_0_), channel_id=1, source_target_pairs={{0,1},{32,40},{1,2},{33,41},{2,3},{34,42},{3,4},{35,43},{4,5},{36,... | collective-permute-start | bytes 1572872 | tf_op jit(solution)/shard_map/ppermute | solution.py:108
  50.3 69.0 %copy-start.5 = (bf16[2,512,256]{2,1,0:T(8,128)(2,1)}, bf16[2,512,256]{2,1,0:T(8,128)(2,1)S(1)}, u32[]{:S(2)}) copy-start(bf16[2,512,256]{2,1,0:T(8,128)(2,1)S(1)} %pad_maximum_fusion.1.refs_1_) | copy-start | bytes 1572868
  52.5 33.4 %collective-permute-start.5 = (bf16[512,256]{1,0:T(8,128)(2,1)}, bf16[512,256]{1,0:T(8,128)(2,1)}, u32[]{:S(2)}, u32[]{:S(2)}) collective-permute-start(bf16[512,256]{1,0:T(8,128)(2,1)} %collective-permute-done.3), channel_id=1, source_target_pairs={{32,39},{33,32},{34,33},{35,34},{36,35},{37,36},{38,37},{39,38},{4... | collective-permute-start | bytes 786440 | tf_op jit(solution)/shard_map/ppermute | solution.py:99
  57.8 43.7 %collective-permute-start.10 = (bf16[2,512,256]{2,1,0:T(8,128)(2,1)S(1)}, bf16[2,512,256]{2,1,0:T(8,128)(2,1)S(1)}, u32[]{:S(2)}, u32[]{:S(2)}) collective-permute-start(bf16[2,512,256]{2,1,0:T(8,128)(2,1)S(1)} %pad_maximum_fusion.1.refs_1_), channel_id=1, source_target_pairs={{0,7},{32,56},{1,0},{33,57},{2,1},{34,58},{3,2},{35,59},{4,3},{36,... | collective-permute-start | bytes 1572872 | tf_op jit(solution)/shard_map/ppermute | solution.py:108
  59.8 39.6 %collective-permute-start.8 = (bf16[2,512,256]{2,1,0:T(8,128)(2,1)S(1)}, bf16[2,512,256]{2,1,0:T(8,128)(2,1)S(1)}, u32[]{:S(2)}, u32[]{:S(2)}) collective-permute-start(bf16[2,512,256]{2,1,0:T(8,128)(2,1)S(1)} %pad_maximum_fusion.1.refs_1_), channel_id=1, source_target_pairs={{0,1},{32,40},{1,2},{33,41},{2,3},{34,42},{3,4},{35,43},{4,5},{36,... | collective-permute-start | bytes 1572872 | tf_op jit(solution)/shard_map/ppermute | solution.py:108
  65.0 0.8 copy-start.4
  65.8 59.9 %copy-start.16 = (s32[8,2]{0,1:T(2,128)S(1)}, s32[8,2]{0,1:T(2,128)}, u32[]{:S(2)}) copy-start(s32[8,2]{0,1:T(2,128)} %param.6) | copy-start | bytes 196
  82.8 40.9 %collective-permute-start.13 = (bf16[2,512,256]{2,1,0:T(8,128)(2,1)}, bf16[2,512,256]{2,1,0:T(8,128)(2,1)}, u32[]{:S(2)}, u32[]{:S(2)}) collective-permute-start(bf16[2,512,256]{2,1,0:T(8,128)(2,1)} %shard_map.60), channel_id=1, source_target_pairs={{0,7},{32,56},{1,0},{33,57},{2,1},{34,58},{3,2},{35,59},{4,3},{36,... | collective-permute-start | bytes 1572872 | tf_op jit(solution)/shard_map/ppermute | solution.py:108
  86.0 11.6 %collective-permute-start.6 = (bf16[512,256]{1,0:T(8,128)(2,1)}, bf16[512,256]{1,0:T(8,128)(2,1)S(1)}, u32[]{:S(2)}, u32[]{:S(2)}) collective-permute-start(bf16[512,256]{1,0:T(8,128)(2,1)} %collective-permute-done.4), channel_id=1, source_target_pairs={{32,33},{33,34},{34,35},{35,36},{36,37},{37,38},{38,39},{39,32},{4... | collective-permute-start | bytes 786440 | tf_op jit(solution)/shard_map/ppermute | solution.py:99
  87.9 56.2 %copy-start.9 = (bf16[2,512,256]{2,1,0:T(8,128)(2,1)}, bf16[2,512,256]{2,1,0:T(8,128)(2,1)S(1)}, u32[]{:S(2)}) copy-start(bf16[2,512,256]{2,1,0:T(8,128)(2,1)S(1)} %collective-permute-done.7.refs_4_) | copy-start | bytes 1572868
  87.9 38.3 %collective-permute-start.11 = (bf16[2,512,256]{2,1,0:T(8,128)(2,1)S(1)}, bf16[2,512,256]{2,1,0:T(8,128)(2,1)S(1)}, u32[]{:S(2)}, u32[]{:S(2)}) collective-permute-start(bf16[2,512,256]{2,1,0:T(8,128)(2,1)S(1)} %collective-permute-done.7.refs_4_), channel_id=1, source_target_pairs={{0,1},{32,40},{1,2},{33,41},{2,3},{34,42},{3,4},{35,43},{4,5},{36,... | collective-permute-start | bytes 1572872 | tf_op jit(solution)/shard_map/ppermute | solution.py:108
  99.4 80.7 %copy-start.10 = (bf16[2,512,256]{2,1,0:T(8,128)(2,1)}, bf16[2,512,256]{2,1,0:T(8,128)(2,1)S(1)}, u32[]{:S(2)}) copy-start(bf16[2,512,256]{2,1,0:T(8,128)(2,1)S(1)} %collective-permute-done.8.refs_5_) | copy-start | bytes 1572868
  99.4 48.7 %collective-permute-start.12 = (bf16[2,512,256]{2,1,0:T(8,128)(2,1)S(1)}, bf16[2,512,256]{2,1,0:T(8,128)(2,1)S(1)}, u32[]{:S(2)}, u32[]{:S(2)}) collective-permute-start(bf16[2,512,256]{2,1,0:T(8,128)(2,1)S(1)} %collective-permute-done.8.refs_5_), channel_id=1, source_target_pairs={{0,1},{32,40},{1,2},{33,41},{2,3},{34,42},{3,4},{35,43},{4,5},{36,... | collective-permute-start | bytes 1572872 | tf_op jit(solution)/shard_map/ppermute | solution.py:108
  101.6 0.8 copy-start.6
  119.4 48.5 %collective-permute-start.14 = (bf16[2,512,256]{2,1,0:T(8,128)(2,1)}, bf16[2,512,256]{2,1,0:T(8,128)(2,1)S(1)}, u32[]{:S(2)}, u32[]{:S(2)}) collective-permute-start(bf16[2,512,256]{2,1,0:T(8,128)(2,1)} %shard_map.61), channel_id=1, source_target_pairs={{0,7},{32,56},{1,0},{33,57},{2,1},{34,58},{3,2},{35,59},{4,3},{36,... | collective-permute-start | bytes 1572872 | tf_op jit(solution)/shard_map/ppermute | solution.py:108
  123.7 45.7 %collective-permute-start.17 = (bf16[2,512,256]{2,1,0:T(8,128)(2,1)}, bf16[2,512,256]{2,1,0:T(8,128)(2,1)S(1)}, u32[]{:S(2)}, u32[]{:S(2)}) collective-permute-start(bf16[2,512,256]{2,1,0:T(8,128)(2,1)} %collective-permute-done.13.refs_10_), channel_id=1, source_target_pairs={{0,7},{32,56},{1,0},{33,57},{2,1},{34,58},{3,2},{35,59},{4,3},{36,... | collective-permute-start | bytes 1572872 | tf_op jit(solution)/shard_map/ppermute | solution.py:108
  126.2 0.8 copy-start.7
  144.1 32.4 %collective-permute-start.15 = (bf16[2,512,256]{2,1,0:T(8,128)(2,1)}, bf16[2,512,256]{2,1,0:T(8,128)(2,1)S(1)}, u32[]{:S(2)}, u32[]{:S(2)}) collective-permute-start(bf16[2,512,256]{2,1,0:T(8,128)(2,1)} %shard_map.62), channel_id=1, source_target_pairs={{0,1},{32,40},{1,2},{33,41},{2,3},{34,42},{3,4},{35,43},{4,5},{36,... | collective-permute-start | bytes 1572872 | tf_op jit(solution)/shard_map/ppermute | solution.py:108
  147.4 29.0 %collective-permute-start.19 = (bf16[2,512,256]{2,1,0:T(8,128)(2,1)}, bf16[2,512,256]{2,1,0:T(8,128)(2,1)S(1)}, u32[]{:S(2)}, u32[]{:S(2)}) collective-permute-start(bf16[2,512,256]{2,1,0:T(8,128)(2,1)} %copy-done.7), channel_id=1, source_target_pairs={{0,2},{1,3},{2,4},{3,5},{4,6},{5,7},{6,0},{7,1},{8,10},{9,11},{10,... | collective-permute-start | bytes 1572872 | tf_op jit(solution)/shard_map/ppermute | solution.py:108
  148.2 0.8 copy-start.8
  166.0 14.1 %collective-permute-start.16 = (bf16[2,512,256]{2,1,0:T(8,128)(2,1)}, bf16[2,512,256]{2,1,0:T(8,128)(2,1)S(1)}, u32[]{:S(2)}, u32[]{:S(2)}) collective-permute-start(bf16[2,512,256]{2,1,0:T(8,128)(2,1)} %shard_map.63), channel_id=1, source_target_pairs={{0,1},{32,40},{1,2},{33,41},{2,3},{34,42},{3,4},{35,43},{4,5},{36,... | collective-permute-start | bytes 1572872 | tf_op jit(solution)/shard_map/ppermute | solution.py:108
  167.9 12.2 %copy-start.11 = (bf16[2,512,256]{2,1,0:T(8,128)(2,1)}, bf16[2,512,256]{2,1,0:T(8,128)(2,1)S(1)}, u32[]{:S(2)}) copy-start(bf16[2,512,256]{2,1,0:T(8,128)(2,1)S(1)} %collective-permute-done.14.refs_11_) | copy-start | bytes 1572868
  167.9 8.6 %collective-permute-start.20 = (bf16[2,512,256]{2,1,0:T(8,128)(2,1)S(1)}, bf16[2,512,256]{2,1,0:T(8,128)(2,1)}, u32[]{:S(2)}, u32[]{:S(2)}) collective-permute-start(bf16[2,512,256]{2,1,0:T(8,128)(2,1)S(1)} %collective-permute-done.14.refs_11_), channel_id=1, source_target_pairs={{0,6},{1,7},{2,0},{3,1},{4,2},{5,3},{6,4},{7,5},{8,14},{9,15},{10,... | collective-permute-start | bytes 1572872 | tf_op jit(solution)/shard_map/ppermute | solution.py:108
  169.4 10.7 %copy-start.12 = (bf16[2,512,256]{2,1,0:T(8,128)(2,1)}, bf16[2,512,256]{2,1,0:T(8,128)(2,1)S(1)}, u32[]{:S(2)}) copy-start(bf16[2,512,256]{2,1,0:T(8,128)(2,1)S(1)} %collective-permute-done.17.refs_14_) | copy-start | bytes 1572868
  169.4 10.7 %collective-permute-start.18 = (bf16[2,512,256]{2,1,0:T(8,128)(2,1)S(1)}, bf16[2,512,256]{2,1,0:T(8,128)(2,1)}, u32[]{:S(2)}, u32[]{:S(2)}) collective-permute-start(bf16[2,512,256]{2,1,0:T(8,128)(2,1)S(1)} %collective-permute-done.14.refs_11_), channel_id=1, source_target_pairs={{0,7},{32,56},{1,0},{33,57},{2,1},{34,58},{3,2},{35,59},{4,3},{36,... | collective-permute-start | bytes 1572872 | tf_op jit(solution)/shard_map/ppermute | solution.py:108
  176.5 3.6 %copy-start.13 = (bf16[2,512,256]{2,1,0:T(8,128)(2,1)}, bf16[2,512,256]{2,1,0:T(8,128)(2,1)S(1)}, u32[]{:S(2)}) copy-start(bf16[2,512,256]{2,1,0:T(8,128)(2,1)S(1)} %collective-permute-done.15.refs_12_) | copy-start | bytes 1572868
  176.5 3.6 %copy-start.14 = (bf16[2,512,256]{2,1,0:T(8,128)(2,1)}, bf16[2,512,256]{2,1,0:T(8,128)(2,1)S(1)}, u32[]{:S(2)}) copy-start(bf16[2,512,256]{2,1,0:T(8,128)(2,1)S(1)} %collective-permute-done.19.refs_16_) | copy-start | bytes 1572868
  180.1 0.8 copy-start.15
  186.2 1.3 copy-start
  187.5 15.6 %all-to-all-start.1 = ((bf16[8,64,512]{2,1,0:T(8,128)(2,1)}), bf16[8,64,512]{2,1,0:T(8,128)(2,1)S(1)}, u32[]{:S(2)}, u32[]{:S(2)}) async-start(bf16[8,64,512]{2,1,0:T(8,128)(2,1)} %get-tuple-element.8), calls=%async_computation.1 | async-start | bytes 1048576 | tf_op jit(solution)/shard_map/all_to_all | solution.py:351
  218.8 13.8 %collective-permute-start.21 = (bf16[8,64,256]{2,1,0:T(8,128)(2,1)S(1)}, bf16[8,64,256]{2,1,0:T(8,128)(2,1)S(1)}, u32[]{:S(2)}, u32[]{:S(2)}) collective-permute-start(bf16[8,64,256]{2,1,0:T(8,128)(2,1)S(1)} %shard_map.66.own_ref), channel_id=1, source_target_pairs={{0,32},{32,0},{1,33},{33,1},{2,34},{34,2},{3,35},{35,3},{4,36},{36... | collective-permute-start | bytes 786440 | tf_op jit(solution)/shard_map/ppermute | solution.py:381
  234.0 52.2 %copy-start.1 = (bf16[8,512,256]{2,1,0:T(8,128)(2,1)S(1)}, bf16[8,512,256]{2,1,0:T(8,128)(2,1)}, u32[]{:S(2)}) copy-start(bf16[8,512,256]{2,1,0:T(8,128)(2,1)} %copy-done) | copy-start | bytes 6291460
  287.6 4.2 %collective-permute-start.22 = (bf16[8,64,128]{2,1,0:T(8,128)(2,1)S(1)}, bf16[8,64,128]{2,1,0:T(8,128)(2,1)S(1)}, u32[]{:S(2)}, u32[]{:S(2)}) collective-permute-start(bf16[8,64,128]{2,1,0:T(8,128)(2,1)S(1)} %get-tuple-element.13), channel_id=1, source_target_pairs={{0,32},{32,0},{1,33},{33,1},{2,34},{34,2},{3,35},{35,3},{4,36},{36... | collective-permute-start | bytes 393224 | tf_op jit(solution)/shard_map/ppermute | solution.py:396
where the time goes:
time: 294 us; the launch traced here: 293 us
  Pallas kernels  84.8 us (29%)
  blocking collectives  84.3 us (29%)
  starting transfers between devices  79 us (27%)
  waiting for transfers between devices  29.4 us (10%)
  other arithmetic  7.67 us (3%)
  local copies, waits for them, and re-layouts  6.13 us (2%)
    all_to_all x4, blocking collectives, exchange(): return lax.all_to_all(x, 'z', 0, 0, tiled=True)  84.3 us
    pallas_call x4, Pallas kernels, either(): pl.pallas_call(either_kernel, out_shape=jax.ShapeDtypeStruct(low.shape, l...  68 us
    ppermute x14, starting transfers between devices, bundle_send(): return lax.ppermute(value, ('core', 'x', 'y'), pairs)  37 us
    ppermute x7, starting transfers between devices, send(): return lax.ppermute(value, ('core', 'x', 'y'), pairs)  22.7 us
    pallas_call x7, Pallas kernels, call(): pl.pallas_call(kernel, out_shape=out_shape, in_specs=in_specs, out_specs=...  16.8 us
    ppermute x1, starting transfers between devices, local(): other = lax.ppermute(own, 'core', swap)  12.6 us
    all_to_all x1, waiting for transfers between devices, exchange(): return lax.all_to_all(x, 'z', 0, 0, tiled=True)  11.9 us
    ppermute x7, waiting for transfers between devices, send(): return lax.ppermute(value, ('core', 'x', 'y'), pairs)  11.8 us
  transfers between devices with their start and end apart: 24, of which 7 were waited for; matrix products, arithmetic and copies ran while one was open for 2% of the time, Pallas kernels for 23%

commit v1 on v0

--- a/solution.py
+++ b/solution.py
@@ -19,7 +19,7 @@
 DEPTH = PANELS * RANK
 ROWS = 256
 HALF = 128
-BUNDLES = 18
+BUNDLES = 10
 EXTRA = 16
 
 
@@ -64,27 +64,24 @@
     return pltpu.with_memory_space_constraint(x, pltpu.HBM)
 
 
-def either_kernel(side_ref, low_ref, high_ref, o_ref, sem):
+def either_kernel(side_ref, low_ref, high_ref, o_ref):
     @pl.when(side_ref[0] == 0)
     def _():
-        pltpu.make_async_copy(low_ref, o_ref, sem).start()
+        o_ref[...] = low_ref[...]
 
     @pl.when(side_ref[0] != 0)
     def _():
-        pltpu.make_async_copy(high_ref, o_ref, sem).start()
-
-    pltpu.make_async_copy(low_ref, o_ref, sem).wait()
+        o_ref[...] = high_ref[...]
 
 
 def either(low, high):
     side = lax.axis_index("core").astype(jnp.int32).reshape(1)
-    anywhere = pl.BlockSpec(memory_space=pl.ANY)
+    vmem = pl.BlockSpec(memory_space=pltpu.VMEM)
     return pl.pallas_call(
         either_kernel,
         out_shape=jax.ShapeDtypeStruct(low.shape, low.dtype),
-        in_specs=[pl.BlockSpec(memory_space=pltpu.SMEM), anywhere, anywhere],
-        out_specs=anywhere,
-        scratch_shapes=[pltpu.SemaphoreType.DMA(())],
+        in_specs=[pl.BlockSpec(memory_space=pltpu.SMEM), vmem, vmem],
+        out_specs=vmem,
     )(side, low, high)
 
 
@@ -114,21 +111,17 @@
     up3 = send(up2, None, 1)
     down3 = send(down2, None, -1)
     up4 = send(up3, None, 1)
-    near = [jnp.stack([own, up1]), jnp.stack([down1, up2])]
-    far = [jnp.stack([down2, up3]), jnp.stack([down3, up4])]
-    out1, out2, out3, out4, out5, out6 = ([None, None] for _ in range(6))
-    for h in range(2):
-        out1[h] = bundle_send(near[h], 1, 1)
-        out2[h] = bundle_send(near[h], -1, -1)
-    for h in range(2):
-        out3[h] = bundle_send(out1[h], 1, 1)
-        out4[h] = bundle_send(either(out2[h], far[h]), -1, -1)
-    for h in range(2):
-        out5[h] = bundle_send(either(out3[h], far[h]), 1, 1)
-        out6[h] = bundle_send(out4[h], -1, -1)
-    out7 = bundle_send(out3[0], 2, None)
-    out8 = bundle_send(out4[1], -2, None)
-    return (*near, *far, *out1, *out2, *out3, *out4, *out5, *out6, out7, out8)
+    near = jnp.stack([own, up1, down1, up2])
+    far = jnp.stack([down2, up3, down3, up4])
+    out1 = bundle_send(near, 1, 1)
+    out2 = bundle_send(near, -1, -1)
+    out3 = bundle_send(out1, 1, 1)
+    out4 = bundle_send(either(out2, far), -1, -1)
+    out5 = bundle_send(either(out3, far), 1, 1)
+    out6 = bundle_send(out4, -1, -1)
+    out7 = bundle_send(out3[0:2], 2, None)
+    out8 = bundle_send(out4[2:4], -2, None)
+    return near, far, out1, out2, out3, out4, out5, out6, out7, out8
 
 
 def pick(index, *values):
@@ -143,12 +136,12 @@
     dy = (lax.axis_index("y").astype(jnp.int32) - rows % 8) % 8
     lower = lax.axis_index("core") == 0
     place0 = pick(dx, 0, 1, 3, 2)
-    half0 = place0 // 2
-    which0 = pick(dy, 0, 4, 8, 12, 16, 14, 10, 6) + half0
+    across = (dy == 4) & (place0 >= 2)
+    which0 = jnp.where(across, 9, pick(dy, 0, 2, 4, 6, 8, 7, 5, 3))
+    place0 = jnp.where(across, place0 - 2, place0)
     place1 = pick(dy, 0, 1, 3, 1, 3, 2, 0, 2)
-    half1 = place1 // 2
-    which1 = jnp.where((dy <= 2) | (dy == 7), pick(dx, 0, 4, 8, 6), pick(dx, 2, 12, 14, 10)) + half1
-    return jnp.where(lower, which0, which1), jnp.where(lower, place0 - 2 * half0, place1 - 2 * half1)
+    which1 = jnp.where((dy <= 2) | (dy == 7), pick(dx, 0, 2, 4, 3), pick(dx, 1, 6, 7, 5))
+    return jnp.where(lower, which0, which1), jnp.where(lower, place0, place1)
 
 
 def sketch_kernel(first_ref, second_ref, z_ref, probe_ref, *refs):

time: 294 us -> 241 us (0.82)
  the two profiles are of different devices: /device:TPU:1 before, /device:TPU:9 now
where the time goes in v1:
time: 241 us; the launch traced here: 240 us
  blocking collectives  88 us (37%)
  starting transfers between devices  66.1 us (27%)
  waiting for transfers between devices  50.5 us (21%)
  Pallas kernels  22 us (9%)
  local copies, waits for them, and re-layouts  7.88 us (3%)
  other arithmetic  4.66 us (2%)
    all_to_all x4, blocking collectives, exchange(): return lax.all_to_all(x, 'z', 0, 0, tiled=True)  88 us
    ppermute x7, starting transfers between devices, send(): return lax.ppermute(value, ('core', 'x', 'y'), pairs)  21.1 us
    ppermute x8, starting transfers between devices, bundle_send(): return lax.ppermute(value, ('core', 'x', 'y'), pairs)  19.5 us
    ppermute x7, waiting for transfers between devices, send(): return lax.ppermute(value, ('core', 'x', 'y'), pairs)  19 us
    ppermute x1, starting transfers between devices, local(): other = lax.ppermute(own, 'core', swap)  18.7 us
    ppermute x8, waiting for transfers between devices, bundle_send(): return lax.ppermute(value, ('core', 'x', 'y'), pairs)  17.5 us
    pallas_call x7, Pallas kernels, call(): pl.pallas_call(kernel, out_shape=out_shape, in_specs=in_specs, out_specs=...  16.7 us
    all_to_all x1, waiting for transfers between devices, exchange(): return lax.all_to_all(x, 'z', 0, 0, tiled=True)  11.9 us
  transfers between devices with their start and end apart: 18, of which 11 were waited for; matrix products, arithmetic and copies ran while one was open for 3% of the time, Pallas kernels for 2%

profile of v1, /device:TPU:9, one launch (start us, length us, event | category | flops | bytes accessed | tf_op | source)
XLA Modules:
  0.0 240.1 jit_solution(4853086522435339914)
XLA Ops:
  0.6 0.7 copy-done.2
  1.4 0.9 shard_map.59
  2.3 23.4 %all_to_all.25 = bf16[8,64,384]{2,1,0:T(8,128)(2,1)S(1)} all-to-all(bf16[8,64,384]{2,1,0:T(8,128)(2,1)S(1)} %shard_map.59), channel_id=1, replica_groups=mesh['z'=8,'core'=2,'x'=4,'y'=8] {'z'}, dimensions={0} | all-to-all | bytes 786432 | tf_op jit(solution)/shard_map/all_to_all | solution.py:344
  25.8 3.2 %collective-permute-start = (bf16[512,256]{1,0:T(8,128)(2,1)S(1)}, bf16[512,256]{1,0:T(8,128)(2,1)S(1)}, u32[]{:S(2)}, u32[]{:S(2)}) collective-permute-start(bf16[512,256]{1,0:T(8,128)(2,1)S(1)} %bitcast.59), channel_id=1, source_target_pairs={{0,8},{32,33},{1,9},{33,34},{2,10},{34,35},{3,11},{35,36},{4,12},{... | collective-permute-start | bytes 786440 | tf_op jit(solution)/shard_map/ppermute | solution.py:96
  29.0 2.1 collective-permute-start.1
  31.1 1.8 collective-permute-done
  32.9 3.2 %collective-permute-start.2 = (bf16[512,256]{1,0:T(8,128)(2,1)S(1)}, bf16[512,256]{1,0:T(8,128)(2,1)S(1)}, u32[]{:S(2)}, u32[]{:S(2)}) collective-permute-start(bf16[512,256]{1,0:T(8,128)(2,1)S(1)} %collective-permute-done), channel_id=1, source_target_pairs={{0,8},{32,33},{1,9},{33,34},{2,10},{34,35},{3,11},{35,36},{4,12},{... | collective-permute-start | bytes 786440 | tf_op jit(solution)/shard_map/ppermute | solution.py:96
  36.4 4.3 %collective-permute-done.2 = bf16[512,256]{1,0:T(8,128)(2,1)S(1)} collective-permute-done((bf16[512,256]{1,0:T(8,128)(2,1)S(1)}, bf16[512,256]{1,0:T(8,128)(2,1)S(1)}, u32[]{:S(2)}, u32[]{:S(2)}) %collective-permute-start.2) | collective-permute-done | bytes 262176 | tf_op jit(solution)/shard_map/ppermute | solution.py:96
  40.9 4.1 %collective-permute-start.8 = (bf16[4,512,256]{2,1,0:T(8,128)(2,1)S(1)}, bf16[4,512,256]{2,1,0:T(8,128)(2,1)S(1)}, u32[]{:S(2)}, u32[]{:S(2)}) collective-permute-start(bf16[4,512,256]{2,1,0:T(8,128)(2,1)S(1)} %pad_maximum_fusion.refs_0_), channel_id=1, source_target_pairs={{0,7},{32,56},{1,0},{33,57},{2,1},{34,58},{3,2},{35,59},{4,3},{36,... | collective-permute-start | bytes 3145736 | tf_op jit(solution)/shard_map/ppermute | solution.py:105
  45.0 1.9 collective-permute-start.7
  46.9 4.6 %collective-permute-start.3 = (bf16[512,256]{1,0:T(8,128)(2,1)S(1)}, bf16[512,256]{1,0:T(8,128)(2,1)S(1)}, u32[]{:S(2)}, u32[]{:S(2)}) collective-permute-start(bf16[512,256]{1,0:T(8,128)(2,1)S(1)} %collective-permute-done.1), channel_id=1, source_target_pairs={{32,39},{33,32},{34,33},{35,34},{36,35},{37,36},{38,37},{39,38},{4... | collective-permute-start | bytes 786440 | tf_op jit(solution)/shard_map/ppermute | solution.py:96
  51.5 1.9 collective-permute-start.4
  53.4 4.2 %collective-permute-done.3 = bf16[512,256]{1,0:T(8,128)(2,1)S(1)} collective-permute-done((bf16[512,256]{1,0:T(8,128)(2,1)S(1)}, bf16[512,256]{1,0:T(8,128)(2,1)S(1)}, u32[]{:S(2)}, u32[]{:S(2)}) %collective-permute-start.3) | collective-permute-done | bytes 262176 | tf_op jit(solution)/shard_map/ppermute | solution.py:96
  57.6 4.2 %collective-permute-start.5 = (bf16[512,256]{1,0:T(8,128)(2,1)S(1)}, bf16[512,256]{1,0:T(8,128)(2,1)S(1)}, u32[]{:S(2)}, u32[]{:S(2)}) collective-permute-start(bf16[512,256]{1,0:T(8,128)(2,1)S(1)} %collective-permute-done.3), channel_id=1, source_target_pairs={{32,39},{33,32},{34,33},{35,34},{36,35},{37,36},{38,37},{39,38},{4... | collective-permute-start | bytes 786440 | tf_op jit(solution)/shard_map/ppermute | solution.py:96
  61.8 1.9 collective-permute-start.6
  63.8 4.7 %collective-permute-done.5 = bf16[512,256]{1,0:T(8,128)(2,1)S(1)} collective-permute-done((bf16[512,256]{1,0:T(8,128)(2,1)S(1)}, bf16[512,256]{1,0:T(8,128)(2,1)S(1)}, u32[]{:S(2)}, u32[]{:S(2)}) %collective-permute-start.5) | collective-permute-done | bytes 262176 | tf_op jit(solution)/shard_map/ppermute | solution.py:96
  68.5 3.7 %collective-permute-done.6 = bf16[512,256]{1,0:T(8,128)(2,1)S(1)} collective-permute-done((bf16[512,256]{1,0:T(8,128)(2,1)S(1)}, bf16[512,256]{1,0:T(8,128)(2,1)S(1)}, u32[]{:S(2)}, u32[]{:S(2)}) %collective-permute-start.6) | collective-permute-done | bytes 262176 | tf_op jit(solution)/shard_map/ppermute | solution.py:96
  72.1 1.1 pad_maximum_fusion.1.high_ref.refs_1_
  73.2 1.0 copy-done.5
  74.2 2.6 %shard_map.60 = bf16[4,512,256]{2,1,0:T(8,128)(2,1)} custom-call(s32[1]{0:T(128)} %bitcast.side_ref, bf16[4,512,256]{2,1,0:T(8,128)(2,1)} %copy-done.5, bf16[4,512,256]{2,1,0:T(8,128)(2,1)} %pad_maximum_fusion.1.high_ref.refs_1_), custom_call_target="tpu_custom_call" | custom-call | tf_op jit(solution)/shard_map/pallas_call | solution.py:80
  76.8 2.2 collective-permute-start.10
  79.0 3.1 %collective-permute-start.9 = (bf16[4,512,256]{2,1,0:T(8,128)(2,1)}, bf16[4,512,256]{2,1,0:T(8,128)(2,1)S(1)}, u32[]{:S(2)}, u32[]{:S(2)}) collective-permute-start(bf16[4,512,256]{2,1,0:T(8,128)(2,1)} %collective-permute-done.7.refs_2_), channel_id=1, source_target_pairs={{0,1},{32,40},{1,2},{33,41},{2,3},{34,42},{3,4},{35,43},{4,5},{36,... | collective-permute-start | bytes 3145736 | tf_op jit(solution)/shard_map/ppermute | solution.py:105
  82.1 10.7 %collective-permute-done.10.refs_5_ = bf16[4,512,256]{2,1,0:T(8,128)(2,1)S(1)} collective-permute-done((bf16[4,512,256]{2,1,0:T(8,128)(2,1)}, bf16[4,512,256]{2,1,0:T(8,128)(2,1)S(1)}, u32[]{:S(2)}, u32[]{:S(2)}) %collective-permute-start.10) | collective-permute-done | bytes 1048608 | tf_op jit(solution)/shard_map/ppermute | solution.py:105
  92.9 3.1 %collective-permute-start.12 = (bf16[4,512,256]{2,1,0:T(8,128)(2,1)S(1)}, bf16[4,512,256]{2,1,0:T(8,128)(2,1)S(1)}, u32[]{:S(2)}, u32[]{:S(2)}) collective-permute-start(bf16[4,512,256]{2,1,0:T(8,128)(2,1)S(1)} %collective-permute-done.10.refs_5_), channel_id=1, source_target_pairs={{0,7},{32,56},{1,0},{33,57},{2,1},{34,58},{3,2},{35,59},{4,3},{36,... | collective-permute-start | bytes 3145736 | tf_op jit(solution)/shard_map/ppermute | solution.py:105
  96.0 1.0 copy-done.3
  97.0 2.7 %shard_map.61 = bf16[4,512,256]{2,1,0:T(8,128)(2,1)} custom-call(s32[1]{0:T(128)} %bitcast.side_ref, bf16[4,512,256]{2,1,0:T(8,128)(2,1)} %copy-done.3, bf16[4,512,256]{2,1,0:T(8,128)(2,1)} %pad_maximum_fusion.1.high_ref.refs_1_), custom_call_target="tpu_custom_call" | custom-call | tf_op jit(solution)/shard_map/pallas_call | solution.py:80
  99.7 2.2 collective-permute-start.11
  101.9 0.9 slice.34
  102.7 1.5 collective-permute-start.14
  104.3 1.9 slice.33
  106.1 1.5 collective-permute-start.13
  107.6 1.3 broadcast_select_fusion.1
  110.2 6.7 %collective-permute-done.11.refs_6_ = bf16[4,512,256]{2,1,0:T(8,128)(2,1)S(1)} collective-permute-done((bf16[4,512,256]{2,1,0:T(8,128)(2,1)}, bf16[4,512,256]{2,1,0:T(8,128)(2,1)S(1)}, u32[]{:S(2)}, u32[]{:S(2)}) %collective-permute-start.11) | collective-permute-done | bytes 1048608 | tf_op jit(solution)/shard_map/ppermute | solution.py:105
  116.9 1.1 copy-done.8
  118.0 5.2 %shard_map.62 = (bf16[8,64,512]{2,1,0:T(8,128)(2,1)}, bf16[8,512,256]{2,1,0:T(8,128)(2,1)S(1)}, bf16[8,512,256]{2,1,0:T(8,128)(2,1)S(1)}) custom-call(s32[2,8]{1,0:T(2,128)S(1)} %pad_add_fusion.first_ref, s32[2,8]{1,0:T(2,128)S(1)} %pad_add_fusion.1.second_ref, s32[1]{0:T(128)} %bitcast.3.z_ref, bf16[8,64,2048]{2,1,0:T(8,128)(2,1)} %bitcast.58, ...), custom_call_target="tpu_custom_call" | custom-call | tf_op jit(solution)/shard_map/pallas_call | solution.py:331
  123.2 1.3 copy-done
  124.5 3.5 %all-to-all-start.1 = ((bf16[8,64,512]{2,1,0:T(8,128)(2,1)}), bf16[8,64,512]{2,1,0:T(8,128)(2,1)S(1)}, u32[]{:S(2)}, u32[]{:S(2)}) async-start(bf16[8,64,512]{2,1,0:T(8,128)(2,1)} %get-tuple-element.8), calls=%async_computation.1 | async-start | bytes 1048576 | tf_op jit(solution)/shard_map/all_to_all | solution.py:344
  128.2 11.9 %all-to-all-done.1.part_ref = bf16[8,64,512]{2,1,0:T(8,128)(2,1)S(1)} async-done(((bf16[8,64,512]{2,1,0:T(8,128)(2,1)}), bf16[8,64,512]{2,1,0:T(8,128)(2,1)S(1)}, u32[]{:S(2)}, u32[]{:S(2)}) %all-to-all-start.1) | async-done | bytes 524320 | tf_op jit(solution)/shard_map/all_to_all | solution.py:344
  140.8 19.1 %all_to_all.26.core_ref = bf16[8,64,512]{2,1,0:T(8,128)(2,1)S(1)} all-to-all(bf16[8,64,512]{2,1,0:T(8,128)(2,1)S(1)} %shard_map.63), channel_id=1, replica_groups=mesh['z'=8,'core'=2,'x'=4,'y'=8] {'z'}, dimensions={0} | all-to-all | bytes 1048576 | tf_op jit(solution)/shard_map/all_to_all | solution.py:344
  160.3 18.7 %collective-permute-start.15 = (bf16[8,64,256]{2,1,0:T(8,128)(2,1)S(1)}, bf16[8,64,256]{2,1,0:T(8,128)(2,1)S(1)}, u32[]{:S(2)}, u32[]{:S(2)}) collective-permute-start(bf16[8,64,256]{2,1,0:T(8,128)(2,1)S(1)} %shard_map.64.own_ref), channel_id=1, source_target_pairs={{0,32},{32,0},{1,33},{33,1},{2,34},{34,2},{3,35},{35,3},{4,36},{36... | collective-permute-start | bytes 786440 | tf_op jit(solution)/shard_map/ppermute | solution.py:374
  179.0 1.1 collective-permute-done.15.other_ref
  180.2 1.4 shard_map.65
  181.6 23.3 %all_to_all.27.part_ref = bf16[8,80,512]{2,1,0:T(8,128)(2,1)S(1)} all-to-all(bf16[8,80,512]{2,1,0:T(8,128)(2,1)S(1)} %shard_map.65), channel_id=1, replica_groups=mesh['z'=8,'core'=2,'x'=4,'y'=8] {'z'}, dimensions={0} | all-to-all | bytes 1310720 | tf_op jit(solution)/shard_map/all_to_all | solution.py:344
  204.9 6.6 %shard_map.66 = bf16[8,80,512]{2,1,0:T(8,128)(2,1)S(1)} custom-call(bf16[8,80,512]{2,1,0:T(8,128)(2,1)S(1)} %all_to_all.27.part_ref, f32[8,64,64]{2,1,0:T(8,128)S(1)} %slice_add_fusion.cores_ref), custom_call_target="tpu_custom_call" | custom-call | tf_op jit(solution)/shard_map/pallas_call | solution.py:331
  211.5 22.3 %all_to_all.28.core_ref = bf16[8,80,512]{2,1,0:T(8,128)(2,1)S(1)} all-to-all(bf16[8,80,512]{2,1,0:T(8,128)(2,1)S(1)} %shard_map.66), channel_id=1, replica_groups=mesh['z'=8,'core'=2,'x'=4,'y'=8] {'z'}, dimensions={0} | all-to-all | bytes 1310720 | tf_op jit(solution)/shard_map/all_to_all | solution.py:344
  233.7 1.4 shard_map.67
  235.1 3.3 %collective-permute-start.16 = (bf16[8,64,128]{2,1,0:T(8,128)(2,1)S(1)}, bf16[8,64,128]{2,1,0:T(8,128)(2,1)S(1)}, u32[]{:S(2)}, u32[]{:S(2)}) collective-permute-start(bf16[8,64,128]{2,1,0:T(8,128)(2,1)S(1)} %get-tuple-element.13), channel_id=1, source_target_pairs={{0,32},{32,0},{1,33},{33,1},{2,34},{34,2},{3,35},{35,3},{4,36},{36... | collective-permute-start | bytes 393224 | tf_op jit(solution)/shard_map/ppermute | solution.py:389
  238.4 1.0 collective-permute-done.16
  (31 shorter events, 3.8 us)
Async XLA Ops:
  0.6 0.8 copy-start.2
  25.8 7.1 %collective-permute-start = (bf16[512,256]{1,0:T(8,128)(2,1)S(1)}, bf16[512,256]{1,0:T(8,128)(2,1)S(1)}, u32[]{:S(2)}, u32[]{:S(2)}) collective-permute-start(bf16[512,256]{1,0:T(8,128)(2,1)S(1)} %bitcast.59), channel_id=1, source_target_pairs={{0,8},{32,33},{1,9},{33,34},{2,10},{34,35},{3,11},{35,36},{4,12},{... | collective-permute-start | bytes 786440 | tf_op jit(solution)/shard_map/ppermute | solution.py:96
  29.0 7.4 %collective-permute-start.1 = (bf16[512,256]{1,0:T(8,128)(2,1)S(1)}, bf16[512,256]{1,0:T(8,128)(2,1)S(1)}, u32[]{:S(2)}, u32[]{:S(2)}) collective-permute-start(bf16[512,256]{1,0:T(8,128)(2,1)S(1)} %bitcast.60), channel_id=1, source_target_pairs={{0,24},{32,39},{1,25},{33,32},{2,26},{34,33},{3,27},{35,34},{4,28}... | collective-permute-start | bytes 786440 | tf_op jit(solution)/shard_map/ppermute | solution.py:96
  32.9 7.9 %collective-permute-start.2 = (bf16[512,256]{1,0:T(8,128)(2,1)S(1)}, bf16[512,256]{1,0:T(8,128)(2,1)S(1)}, u32[]{:S(2)}, u32[]{:S(2)}) collective-permute-start(bf16[512,256]{1,0:T(8,128)(2,1)S(1)} %collective-permute-done), channel_id=1, source_target_pairs={{0,8},{32,33},{1,9},{33,34},{2,10},{34,35},{3,11},{35,36},{4,12},{... | collective-permute-start | bytes 786440 | tf_op jit(solution)/shard_map/ppermute | solution.py:96
  40.9 36.0 %copy-start.4 = (bf16[4,512,256]{2,1,0:T(8,128)(2,1)}, bf16[4,512,256]{2,1,0:T(8,128)(2,1)S(1)}, u32[]{:S(2)}) copy-start(bf16[4,512,256]{2,1,0:T(8,128)(2,1)S(1)} %pad_maximum_fusion.refs_0_) | copy-start | bytes 3145732
  40.9 32.4 %collective-permute-start.8 = (bf16[4,512,256]{2,1,0:T(8,128)(2,1)S(1)}, bf16[4,512,256]{2,1,0:T(8,128)(2,1)S(1)}, u32[]{:S(2)}, u32[]{:S(2)}) collective-permute-start(bf16[4,512,256]{2,1,0:T(8,128)(2,1)S(1)} %pad_maximum_fusion.refs_0_), channel_id=1, source_target_pairs={{0,7},{32,56},{1,0},{33,57},{2,1},{34,58},{3,2},{35,59},{4,3},{36,... | collective-permute-start | bytes 3145736 | tf_op jit(solution)/shard_map/ppermute | solution.py:105
  45.0 34.0 %collective-permute-start.7 = (bf16[4,512,256]{2,1,0:T(8,128)(2,1)S(1)}, bf16[4,512,256]{2,1,0:T(8,128)(2,1)}, u32[]{:S(2)}, u32[]{:S(2)}) collective-permute-start(bf16[4,512,256]{2,1,0:T(8,128)(2,1)S(1)} %pad_maximum_fusion.refs_0_), channel_id=1, source_target_pairs={{0,1},{32,40},{1,2},{33,41},{2,3},{34,42},{3,4},{35,43},{4,5},{36,... | collective-permute-start | bytes 3145736 | tf_op jit(solution)/shard_map/ppermute | solution.py:105
  46.9 10.7 %collective-permute-start.3 = (bf16[512,256]{1,0:T(8,128)(2,1)S(1)}, bf16[512,256]{1,0:T(8,128)(2,1)S(1)}, u32[]{:S(2)}, u32[]{:S(2)}) collective-permute-start(bf16[512,256]{1,0:T(8,128)(2,1)S(1)} %collective-permute-done.1), channel_id=1, source_target_pairs={{32,39},{33,32},{34,33},{35,34},{36,35},{37,36},{38,37},{39,38},{4... | collective-permute-start | bytes 786440 | tf_op jit(solution)/shard_map/ppermute | solution.py:96
  51.5 10.3 %collective-permute-start.4 = (bf16[512,256]{1,0:T(8,128)(2,1)S(1)}, bf16[512,256]{1,0:T(8,128)(2,1)S(1)}, u32[]{:S(2)}, u32[]{:S(2)}) collective-permute-start(bf16[512,256]{1,0:T(8,128)(2,1)S(1)} %collective-permute-done.2), channel_id=1, source_target_pairs={{32,33},{33,34},{34,35},{35,36},{36,37},{37,38},{38,39},{39,32},{4... | collective-permute-start | bytes 786440 | tf_op jit(solution)/shard_map/ppermute | solution.py:96
  57.6 10.9 %collective-permute-start.5 = (bf16[512,256]{1,0:T(8,128)(2,1)S(1)}, bf16[512,256]{1,0:T(8,128)(2,1)S(1)}, u32[]{:S(2)}, u32[]{:S(2)}) collective-permute-start(bf16[512,256]{1,0:T(8,128)(2,1)S(1)} %collective-permute-done.3), channel_id=1, source_target_pairs={{32,39},{33,32},{34,33},{35,34},{36,35},{37,36},{38,37},{39,38},{4... | collective-permute-start | bytes 786440 | tf_op jit(solution)/shard_map/ppermute | solution.py:96
  61.8 10.3 %collective-permute-start.6 = (bf16[512,256]{1,0:T(8,128)(2,1)S(1)}, bf16[512,256]{1,0:T(8,128)(2,1)S(1)}, u32[]{:S(2)}, u32[]{:S(2)}) collective-permute-start(bf16[512,256]{1,0:T(8,128)(2,1)S(1)} %collective-permute-done.4), channel_id=1, source_target_pairs={{32,33},{33,34},{34,35},{35,36},{36,37},{37,38},{38,39},{39,32},{4... | collective-permute-start | bytes 786440 | tf_op jit(solution)/shard_map/ppermute | solution.py:96
  73.2 1.0 copy-start.5
  76.8 16.0 %collective-permute-start.10 = (bf16[4,512,256]{2,1,0:T(8,128)(2,1)}, bf16[4,512,256]{2,1,0:T(8,128)(2,1)S(1)}, u32[]{:S(2)}, u32[]{:S(2)}) collective-permute-start(bf16[4,512,256]{2,1,0:T(8,128)(2,1)} %shard_map.60), channel_id=1, source_target_pairs={{0,7},{32,56},{1,0},{33,57},{2,1},{34,58},{3,2},{35,59},{4,3},{36,... | collective-permute-start | bytes 3145736 | tf_op jit(solution)/shard_map/ppermute | solution.py:105
  79.0 17.0 %collective-permute-start.9 = (bf16[4,512,256]{2,1,0:T(8,128)(2,1)}, bf16[4,512,256]{2,1,0:T(8,128)(2,1)S(1)}, u32[]{:S(2)}, u32[]{:S(2)}) collective-permute-start(bf16[4,512,256]{2,1,0:T(8,128)(2,1)} %collective-permute-done.7.refs_2_), channel_id=1, source_target_pairs={{0,1},{32,40},{1,2},{33,41},{2,3},{34,42},{3,4},{35,43},{4,5},{36,... | collective-permute-start | bytes 3145736 | tf_op jit(solution)/shard_map/ppermute | solution.py:105
  92.9 24.0 %copy-start.6 = (bf16[4,512,256]{2,1,0:T(8,128)(2,1)}, bf16[4,512,256]{2,1,0:T(8,128)(2,1)S(1)}, u32[]{:S(2)}) copy-start(bf16[4,512,256]{2,1,0:T(8,128)(2,1)S(1)} %collective-permute-done.10.refs_5_) | copy-start | bytes 3145732
  92.9 17.3 %collective-permute-start.12 = (bf16[4,512,256]{2,1,0:T(8,128)(2,1)S(1)}, bf16[4,512,256]{2,1,0:T(8,128)(2,1)S(1)}, u32[]{:S(2)}, u32[]{:S(2)}) collective-permute-start(bf16[4,512,256]{2,1,0:T(8,128)(2,1)S(1)} %collective-permute-done.10.refs_5_), channel_id=1, source_target_pairs={{0,7},{32,56},{1,0},{33,57},{2,1},{34,58},{3,2},{35,59},{4,3},{36,... | collective-permute-start | bytes 3145736 | tf_op jit(solution)/shard_map/ppermute | solution.py:105
  96.0 1.0 copy-start.3
  99.7 17.2 %collective-permute-start.11 = (bf16[4,512,256]{2,1,0:T(8,128)(2,1)}, bf16[4,512,256]{2,1,0:T(8,128)(2,1)S(1)}, u32[]{:S(2)}, u32[]{:S(2)}) collective-permute-start(bf16[4,512,256]{2,1,0:T(8,128)(2,1)} %shard_map.61), channel_id=1, source_target_pairs={{0,1},{32,40},{1,2},{33,41},{2,3},{34,42},{3,4},{35,43},{4,5},{36,... | collective-permute-start | bytes 3145736 | tf_op jit(solution)/shard_map/ppermute | solution.py:105
  102.7 7.4 %collective-permute-start.14 = (bf16[2,512,256]{2,1,0:T(8,128)(2,1)}, bf16[2,512,256]{2,1,0:T(8,128)(2,1)}, u32[]{:S(2)}, u32[]{:S(2)}) collective-permute-start(bf16[2,512,256]{2,1,0:T(8,128)(2,1)} %slice.34), channel_id=1, source_target_pairs={{0,6},{1,7},{2,0},{3,1},{4,2},{5,3},{6,4},{7,5},{8,14},{9,15},{10,... | collective-permute-start | bytes 1572872 | tf_op jit(solution)/shard_map/ppermute | solution.py:105
  106.1 4.0 %collective-permute-start.13 = (bf16[2,512,256]{2,1,0:T(8,128)(2,1)}, bf16[2,512,256]{2,1,0:T(8,128)(2,1)}, u32[]{:S(2)}, u32[]{:S(2)}) collective-permute-start(bf16[2,512,256]{2,1,0:T(8,128)(2,1)} %slice.33), channel_id=1, source_target_pairs={{0,2},{1,3},{2,4},{3,5},{4,6},{5,7},{6,0},{7,1},{8,10},{9,11},{10,... | collective-permute-start | bytes 1572872 | tf_op jit(solution)/shard_map/ppermute | solution.py:105
  110.1 6.7 %copy-start.7 = (bf16[4,512,256]{2,1,0:T(8,128)(2,1)}, bf16[4,512,256]{2,1,0:T(8,128)(2,1)S(1)}, u32[]{:S(2)}) copy-start(bf16[4,512,256]{2,1,0:T(8,128)(2,1)S(1)} %collective-permute-done.12.refs_7_) | copy-start | bytes 3145732
  116.9 1.1 copy-start.8
  123.2 1.3 copy-start
  124.5 15.6 %all-to-all-start.1 = ((bf16[8,64,512]{2,1,0:T(8,128)(2,1)}), bf16[8,64,512]{2,1,0:T(8,128)(2,1)S(1)}, u32[]{:S(2)}, u32[]{:S(2)}) async-start(bf16[8,64,512]{2,1,0:T(8,128)(2,1)} %get-tuple-element.8), calls=%async_computation.1 | async-start | bytes 1048576 | tf_op jit(solution)/shard_map/all_to_all | solution.py:344
  160.3 19.8 %collective-permute-start.15 = (bf16[8,64,256]{2,1,0:T(8,128)(2,1)S(1)}, bf16[8,64,256]{2,1,0:T(8,128)(2,1)S(1)}, u32[]{:S(2)}, u32[]{:S(2)}) collective-permute-start(bf16[8,64,256]{2,1,0:T(8,128)(2,1)S(1)} %shard_map.64.own_ref), channel_id=1, source_target_pairs={{0,32},{32,0},{1,33},{33,1},{2,34},{34,2},{3,35},{35,3},{4,36},{36... | collective-permute-start | bytes 786440 | tf_op jit(solution)/shard_map/ppermute | solution.py:374
  181.6 52.1 %copy-start.1 = (bf16[8,512,256]{2,1,0:T(8,128)(2,1)S(1)}, bf16[8,512,256]{2,1,0:T(8,128)(2,1)}, u32[]{:S(2)}) copy-start(bf16[8,512,256]{2,1,0:T(8,128)(2,1)} %copy-done) | copy-start | bytes 6291460
  235.1 4.2 %collective-permute-start.16 = (bf16[8,64,128]{2,1,0:T(8,128)(2,1)S(1)}, bf16[8,64,128]{2,1,0:T(8,128)(2,1)S(1)}, u32[]{:S(2)}, u32[]{:S(2)}) collective-permute-start(bf16[8,64,128]{2,1,0:T(8,128)(2,1)S(1)} %get-tuple-element.13), channel_id=1, source_target_pairs={{0,32},{32,0},{1,33},{33,1},{2,34},{34,2},{3,35},{35,3},{4,36},{36... | collective-permute-start | bytes 393224 | tf_op jit(solution)/shard_map/ppermute | solution.py:389

commit v2 on v0

--- a/solution.py
+++ b/solution.py
@@ -64,27 +64,24 @@
     return pltpu.with_memory_space_constraint(x, pltpu.HBM)
 
 
-def either_kernel(side_ref, low_ref, high_ref, o_ref, sem):
+def either_kernel(side_ref, low_ref, high_ref, o_ref):
     @pl.when(side_ref[0] == 0)
     def _():
-        pltpu.make_async_copy(low_ref, o_ref, sem).start()
+        o_ref[...] = low_ref[...]
 
     @pl.when(side_ref[0] != 0)
     def _():
-        pltpu.make_async_copy(high_ref, o_ref, sem).start()
-
-    pltpu.make_async_copy(low_ref, o_ref, sem).wait()
+        o_ref[...] = high_ref[...]
 
 
 def either(low, high):
     side = lax.axis_index("core").astype(jnp.int32).reshape(1)
-    anywhere = pl.BlockSpec(memory_space=pl.ANY)
+    vmem = pl.BlockSpec(memory_space=pltpu.VMEM)
     return pl.pallas_call(
         either_kernel,
         out_shape=jax.ShapeDtypeStruct(low.shape, low.dtype),
-        in_specs=[pl.BlockSpec(memory_space=pltpu.SMEM), anywhere, anywhere],
-        out_specs=anywhere,
-        scratch_shapes=[pltpu.SemaphoreType.DMA(())],
+        in_specs=[pl.BlockSpec(memory_space=pltpu.SMEM), vmem, vmem],
+        out_specs=vmem,
     )(side, low, high)
 
 
@@ -102,7 +99,8 @@
         pairs = []
         for x in range(4):
             for y in range(8):
-                pairs.append((x * 8 + y, x * 8 + (y + y_step) % 8))
+                if y_step is not None:
+                    pairs.append((x * 8 + y, x * 8 + (y + y_step) % 8))
                 if x_step is not None:
                     pairs.append((32 + x * 8 + y, 32 + (x + x_step) % 4 * 8 + y))
         return lax.ppermute(value, ("core", "x", "y"), pairs)
@@ -119,16 +117,14 @@
     out1, out2, out3, out4, out5, out6 = ([None, None] for _ in range(6))
     for h in range(2):
         out1[h] = bundle_send(near[h], 1, 1)
-        out2[h] = bundle_send(near[h], -1, -1)
-    for h in range(2):
+        out2[h] = bundle_send(either(near[h], far[h]), -1, -1)
         out3[h] = bundle_send(out1[h], 1, 1)
-        out4[h] = bundle_send(either(out2[h], far[h]), -1, -1)
-    for h in range(2):
-        out5[h] = bundle_send(either(out3[h], far[h]), 1, 1)
+        out4[h] = bundle_send(out2[h], -1, -1)
+        out5[h] = bundle_send(out3[h], 1, 1)
         out6[h] = bundle_send(out4[h], -1, -1)
-    out7 = bundle_send(out3[0], 2, None)
-    out8 = bundle_send(out4[1], -2, None)
-    return (*near, *far, *out1, *out2, *out3, *out4, *out5, *out6, out7, out8)
+    out7 = bundle_send(out5[1], 1, None)
+    out8 = bundle_send(out6[0], -1, None)
+    return (*near, *far, *out1, *out2, *out3, *out4, *out5, *out6, out8, out7)
 
 
 def pick(index, *values):
@@ -147,7 +143,7 @@
     which0 = pick(dy, 0, 4, 8, 12, 16, 14, 10, 6) + half0
     place1 = pick(dy, 0, 1, 3, 1, 3, 2, 0, 2)
     half1 = place1 // 2
-    which1 = jnp.where((dy <= 2) | (dy == 7), pick(dx, 0, 4, 8, 6), pick(dx, 2, 12, 14, 10)) + half1
+    which1 = jnp.where((dy <= 2) | (dy == 7), pick(dx, 0, 4, 8, 12), pick(dx, 2, 14, 10, 6)) + half1
     return jnp.where(lower, which0, which1), jnp.where(lower, place0 - 2 * half0, place1 - 2 * half1)
 
 

time: 294 us -> 226 us (0.77)
  Pallas kernels: 84.8 us -> 21 us
  starting transfers between devices: 79 us -> 74 us
  local copies, waits for them, and re-layouts: 6.13 us -> 2.15 us
    pallas_call x4 -> x2, Pallas kernels: 68 us -> 4.07 us  [either(): pl.pallas_call(either_kernel, out_shape=jax.ShapeDtypeStruct(low.shape, l...]
    ppermute x1, starting transfers between devices: 12.6 us -> 5.98 us  [local(): other = lax.ppermute(own, 'core', swap)]
    unnamed x34 -> x24, local copies, waits for them, and re-layouts: 6.12 us -> 2.14 us
    ppermute x14, starting transfers between devices: 37 us -> 40.6 us  [bundle_send(): return lax.ppermute(value, ('core', 'x', 'y'), pairs)]
    all_to_all x1, waiting for transfers between devices: 11.9 us -> 14.9 us  [exchange(): return lax.all_to_all(x, 'z', 0, 0, tiled=True)]
  transfers between devices with their start and end apart: 24 -> 24, of which waited for: 7 -> 9; matrix products, arithmetic and copies ran while one was open for 2% -> 3% of each run, Pallas kernels for 23% -> 2%
where the time goes in v2:
time: 226 us; the launch traced here: 222 us
  blocking collectives  87.1 us (39%)
  starting transfers between devices  74 us (33%)
  waiting for transfers between devices  30.4 us (13%)
  Pallas kernels  21 us (9%)
  other arithmetic  6.49 us (3%)
    all_to_all x4, blocking collectives, exchange(): return lax.all_to_all(x, 'z', 0, 0, tiled=True)  87.1 us
    ppermute x14, starting transfers between devices, bundle_send(): return lax.ppermute(value, ('core', 'x', 'y'), pairs)  40.6 us
    ppermute x7, starting transfers between devices, send(): return lax.ppermute(value, ('core', 'x', 'y'), pairs)  20.7 us
    pallas_call x7, Pallas kernels, call(): pl.pallas_call(kernel, out_shape=out_shape, in_specs=in_specs, out_specs=...  16.9 us
    all_to_all x1, waiting for transfers between devices, exchange(): return lax.all_to_all(x, 'z', 0, 0, tiled=True)  14.9 us
    ppermute x7, waiting for transfers between devices, send(): return lax.ppermute(value, ('core', 'x', 'y'), pairs)  12.5 us
    ppermute x1, starting transfers between devices, local(): other = lax.ppermute(own, 'core', swap)  5.98 us
  transfers between devices with their start and end apart: 24, of which 9 were waited for; matrix products, arithmetic and copies ran while one was open for 3% of the time, Pallas kernels for 2%

profile of v2, /device:TPU:1, one launch (start us, length us, event | category | flops | bytes accessed | tf_op | source)
XLA Modules:
  0.0 222.2 jit_solution(2508117092299149931)
XLA Ops:
  1.4 0.9 shard_map.59
  2.3 24.2 %all_to_all.25 = bf16[8,64,384]{2,1,0:T(8,128)(2,1)S(1)} all-to-all(bf16[8,64,384]{2,1,0:T(8,128)(2,1)S(1)} %shard_map.59), channel_id=1, replica_groups=mesh['z'=8,'core'=2,'x'=4,'y'=8] {'z'}, dimensions={0} | all-to-all | bytes 786432 | tf_op jit(solution)/shard_map/all_to_all | solution.py:347
  26.6 3.2 %collective-permute-start = (bf16[512,256]{1,0:T(8,128)(2,1)S(1)}, bf16[512,256]{1,0:T(8,128)(2,1)S(1)}, u32[]{:S(2)}, u32[]{:S(2)}) collective-permute-start(bf16[512,256]{1,0:T(8,128)(2,1)S(1)} %bitcast.57), channel_id=1, source_target_pairs={{0,8},{32,33},{1,9},{33,34},{2,10},{34,35},{3,11},{35,36},{4,12},{... | collective-permute-start | bytes 786440 | tf_op jit(solution)/shard_map/ppermute | solution.py:96
  29.8 3.8 %collective-permute-start.1 = (bf16[512,256]{1,0:T(8,128)(2,1)S(1)}, bf16[512,256]{1,0:T(8,128)(2,1)S(1)}, u32[]{:S(2)}, u32[]{:S(2)}) collective-permute-start(bf16[512,256]{1,0:T(8,128)(2,1)S(1)} %bitcast.58), channel_id=1, source_target_pairs={{0,24},{32,39},{1,25},{33,32},{2,26},{34,33},{3,27},{35,34},{4,28}... | collective-permute-start | bytes 786440 | tf_op jit(solution)/shard_map/ppermute | solution.py:96
  33.6 2.1 collective-permute-done
  35.7 1.9 collective-permute-start.2
  37.7 4.6 %collective-permute-start.3 = (bf16[512,256]{1,0:T(8,128)(2,1)S(1)}, bf16[512,256]{1,0:T(8,128)(2,1)S(1)}, u32[]{:S(2)}, u32[]{:S(2)}) collective-permute-start(bf16[512,256]{1,0:T(8,128)(2,1)S(1)} %collective-permute-done.1), channel_id=1, source_target_pairs={{32,39},{33,32},{34,33},{35,34},{36,35},{37,36},{38,37},{39,38},{4... | collective-permute-start | bytes 786440 | tf_op jit(solution)/shard_map/ppermute | solution.py:96
  42.2 1.8 collective-permute-done.2
  44.1 1.9 collective-permute-start.4
  46.0 0.8 pad_maximum_fusion.low_ref.refs_0_
  46.9 3.0 %collective-permute-start.8 = (bf16[2,512,256]{2,1,0:T(8,128)(2,1)S(1)}, bf16[2,512,256]{2,1,0:T(8,128)(2,1)S(1)}, u32[]{:S(2)}, u32[]{:S(2)}) collective-permute-start(bf16[2,512,256]{2,1,0:T(8,128)(2,1)S(1)} %pad_maximum_fusion.1.low_ref.refs_1_), channel_id=1, source_target_pairs={{0,1},{32,40},{1,2},{33,41},{2,3},{34,42},{3,4},{35,43},{4,5},{36,... | collective-permute-start | bytes 1572872 | tf_op jit(solution)/shard_map/ppermute | solution.py:106
  49.8 2.5 %collective-permute-done.4 = bf16[512,256]{1,0:T(8,128)(2,1)S(1)} collective-permute-done((bf16[512,256]{1,0:T(8,128)(2,1)S(1)}, bf16[512,256]{1,0:T(8,128)(2,1)S(1)}, u32[]{:S(2)}, u32[]{:S(2)}) %collective-permute-start.4) | collective-permute-done | bytes 262176 | tf_op jit(solution)/shard_map/ppermute | solution.py:96
  52.4 0.8 pad_maximum_fusion.2.high_ref.refs_2_
  53.2 2.0 shard_map.60
  55.2 4.1 %collective-permute-start.9 = (bf16[2,512,256]{2,1,0:T(8,128)(2,1)}, bf16[2,512,256]{2,1,0:T(8,128)(2,1)S(1)}, u32[]{:S(2)}, u32[]{:S(2)}) collective-permute-start(bf16[2,512,256]{2,1,0:T(8,128)(2,1)} %shard_map.60), channel_id=1, source_target_pairs={{0,7},{32,56},{1,0},{33,57},{2,1},{34,58},{3,2},{35,59},{4,3},{36,... | collective-permute-start | bytes 1572872 | tf_op jit(solution)/shard_map/ppermute | solution.py:106
  59.3 1.9 collective-permute-start.5
  61.3 3.4 %collective-permute-start.6 = (bf16[512,256]{1,0:T(8,128)(2,1)S(1)}, bf16[512,256]{1,0:T(8,128)(2,1)S(1)}, u32[]{:S(2)}, u32[]{:S(2)}) collective-permute-start(bf16[512,256]{1,0:T(8,128)(2,1)S(1)} %collective-permute-done.4), channel_id=1, source_target_pairs={{32,33},{33,34},{34,35},{35,36},{36,37},{37,38},{38,39},{39,32},{4... | collective-permute-start | bytes 786440 | tf_op jit(solution)/shard_map/ppermute | solution.py:96
  64.6 1.9 collective-permute-start.7
  66.6 2.8 %collective-permute-done.5 = bf16[512,256]{1,0:T(8,128)(2,1)S(1)} collective-permute-done((bf16[512,256]{1,0:T(8,128)(2,1)S(1)}, bf16[512,256]{1,0:T(8,128)(2,1)S(1)}, u32[]{:S(2)}, u32[]{:S(2)}) %collective-permute-start.5) | collective-permute-done | bytes 262176 | tf_op jit(solution)/shard_map/ppermute | solution.py:96
  69.4 3.2 %collective-permute-done.6 = bf16[512,256]{1,0:T(8,128)(2,1)S(1)} collective-permute-done((bf16[512,256]{1,0:T(8,128)(2,1)S(1)}, bf16[512,256]{1,0:T(8,128)(2,1)S(1)}, u32[]{:S(2)}, u32[]{:S(2)}) %collective-permute-start.6) | collective-permute-done | bytes 262176 | tf_op jit(solution)/shard_map/ppermute | solution.py:96
  72.6 0.9 pad_maximum_fusion.3.high_ref.refs_3_
  73.5 2.0 shard_map.61
  75.5 2.7 %collective-permute-start.10 = (bf16[2,512,256]{2,1,0:T(8,128)(2,1)}, bf16[2,512,256]{2,1,0:T(8,128)(2,1)S(1)}, u32[]{:S(2)}, u32[]{:S(2)}) collective-permute-start(bf16[2,512,256]{2,1,0:T(8,128)(2,1)} %shard_map.61), channel_id=1, source_target_pairs={{0,7},{32,56},{1,0},{33,57},{2,1},{34,58},{3,2},{35,59},{4,3},{36,... | collective-permute-start | bytes 1572872 | tf_op jit(solution)/shard_map/ppermute | solution.py:106
  78.2 2.6 %collective-permute-start.12 = (bf16[2,512,256]{2,1,0:T(8,128)(2,1)S(1)}, bf16[2,512,256]{2,1,0:T(8,128)(2,1)S(1)}, u32[]{:S(2)}, u32[]{:S(2)}) collective-permute-start(bf16[2,512,256]{2,1,0:T(8,128)(2,1)S(1)} %collective-permute-done.8.refs_5_), channel_id=1, source_target_pairs={{0,1},{32,40},{1,2},{33,41},{2,3},{34,42},{3,4},{35,43},{4,5},{36,... | collective-permute-start | bytes 1572872 | tf_op jit(solution)/shard_map/ppermute | solution.py:106
  80.8 3.9 %collective-permute-start.13 = (bf16[2,512,256]{2,1,0:T(8,128)(2,1)S(1)}, bf16[2,512,256]{2,1,0:T(8,128)(2,1)}, u32[]{:S(2)}, u32[]{:S(2)}) collective-permute-start(bf16[2,512,256]{2,1,0:T(8,128)(2,1)S(1)} %collective-permute-done.9.refs_6_), channel_id=1, source_target_pairs={{0,7},{32,56},{1,0},{33,57},{2,1},{34,58},{3,2},{35,59},{4,3},{36,... | collective-permute-start | bytes 1572872 | tf_op jit(solution)/shard_map/ppermute | solution.py:106
  84.7 1.9 collective-permute-start.11
  86.7 4.6 %collective-permute-start.14 = (bf16[2,512,256]{2,1,0:T(8,128)(2,1)S(1)}, bf16[2,512,256]{2,1,0:T(8,128)(2,1)}, u32[]{:S(2)}, u32[]{:S(2)}) collective-permute-start(bf16[2,512,256]{2,1,0:T(8,128)(2,1)S(1)} %collective-permute-done.10.refs_7_), channel_id=1, source_target_pairs={{0,7},{32,56},{1,0},{33,57},{2,1},{34,58},{3,2},{35,59},{4,3},{36,... | collective-permute-start | bytes 1572872 | tf_op jit(solution)/shard_map/ppermute | solution.py:106
  91.3 1.9 collective-permute-start.16
  93.2 4.6 %collective-permute-start.17 = (bf16[2,512,256]{2,1,0:T(8,128)(2,1)}, bf16[2,512,256]{2,1,0:T(8,128)(2,1)}, u32[]{:S(2)}, u32[]{:S(2)}) collective-permute-start(bf16[2,512,256]{2,1,0:T(8,128)(2,1)} %collective-permute-done.13.refs_10_), channel_id=1, source_target_pairs={{0,7},{32,56},{1,0},{33,57},{2,1},{34,58},{3,2},{35,59},{4,3},{36,... | collective-permute-start | bytes 1572872 | tf_op jit(solution)/shard_map/ppermute | solution.py:106
  98.4 1.9 collective-permute-start.15
  100.3 4.6 %collective-permute-start.18 = (bf16[2,512,256]{2,1,0:T(8,128)(2,1)}, bf16[2,512,256]{2,1,0:T(8,128)(2,1)}, u32[]{:S(2)}, u32[]{:S(2)}) collective-permute-start(bf16[2,512,256]{2,1,0:T(8,128)(2,1)} %collective-permute-done.14.refs_11_), channel_id=1, source_target_pairs={{0,7},{32,56},{1,0},{33,57},{2,1},{34,58},{3,2},{35,59},{4,3},{36,... | collective-permute-start | bytes 1572872 | tf_op jit(solution)/shard_map/ppermute | solution.py:106
  104.9 1.5 collective-permute-start.20
  106.4 1.5 collective-permute-start.19
  110.4 0.9 collective-permute-done.18.refs_15_
  111.4 5.4 %shard_map.62 = (bf16[8,64,512]{2,1,0:T(8,128)(2,1)}, bf16[8,512,256]{2,1,0:T(8,128)(2,1)S(1)}, bf16[8,512,256]{2,1,0:T(8,128)(2,1)S(1)}) custom-call(s32[2,8]{1,0:T(2,128)S(1)} %pad_add_fusion.first_ref, s32[2,8]{1,0:T(2,128)S(1)} %pad_add_fusion.1.second_ref, s32[1]{0:T(128)} %bitcast.3.z_ref, bf16[8,64,2048]{2,1,0:T(8,128)(2,1)} %bitcast.56, ...), custom_call_target="tpu_custom_call" | custom-call | tf_op jit(solution)/shard_map/pallas_call | solution.py:334
  116.8 1.3 copy-done
  118.1 3.5 %all-to-all-start.1 = ((bf16[8,64,512]{2,1,0:T(8,128)(2,1)}), bf16[8,64,512]{2,1,0:T(8,128)(2,1)S(1)}, u32[]{:S(2)}, u32[]{:S(2)}) async-start(bf16[8,64,512]{2,1,0:T(8,128)(2,1)} %get-tuple-element.8), calls=%async_computation.1 | async-start | bytes 1048576 | tf_op jit(solution)/shard_map/all_to_all | solution.py:347
  121.8 14.9 %all-to-all-done.1.part_ref = bf16[8,64,512]{2,1,0:T(8,128)(2,1)S(1)} async-done(((bf16[8,64,512]{2,1,0:T(8,128)(2,1)}), bf16[8,64,512]{2,1,0:T(8,128)(2,1)S(1)}, u32[]{:S(2)}, u32[]{:S(2)}) %all-to-all-start.1) | async-done | bytes 524320 | tf_op jit(solution)/shard_map/all_to_all | solution.py:347
  137.4 17.3 %all_to_all.26.core_ref = bf16[8,64,512]{2,1,0:T(8,128)(2,1)S(1)} all-to-all(bf16[8,64,512]{2,1,0:T(8,128)(2,1)S(1)} %shard_map.63), channel_id=1, replica_groups=mesh['z'=8,'core'=2,'x'=4,'y'=8] {'z'}, dimensions={0} | all-to-all | bytes 1048576 | tf_op jit(solution)/shard_map/all_to_all | solution.py:347
  155.2 6.0 %collective-permute-start.21 = (bf16[8,64,256]{2,1,0:T(8,128)(2,1)S(1)}, bf16[8,64,256]{2,1,0:T(8,128)(2,1)S(1)}, u32[]{:S(2)}, u32[]{:S(2)}) collective-permute-start(bf16[8,64,256]{2,1,0:T(8,128)(2,1)S(1)} %shard_map.64.own_ref), channel_id=1, source_target_pairs={{0,32},{32,0},{1,33},{33,1},{2,34},{34,2},{3,35},{35,3},{4,36},{36... | collective-permute-start | bytes 786440 | tf_op jit(solution)/shard_map/ppermute | solution.py:377
  161.1 1.1 collective-permute-done.21.other_ref
  162.3 1.4 shard_map.65
  163.7 23.3 %all_to_all.27.part_ref = bf16[8,80,512]{2,1,0:T(8,128)(2,1)S(1)} all-to-all(bf16[8,80,512]{2,1,0:T(8,128)(2,1)S(1)} %shard_map.65), channel_id=1, replica_groups=mesh['z'=8,'core'=2,'x'=4,'y'=8] {'z'}, dimensions={0} | all-to-all | bytes 1310720 | tf_op jit(solution)/shard_map/all_to_all | solution.py:347
  187.0 6.6 %shard_map.66 = bf16[8,80,512]{2,1,0:T(8,128)(2,1)S(1)} custom-call(bf16[8,80,512]{2,1,0:T(8,128)(2,1)S(1)} %all_to_all.27.part_ref, f32[8,64,64]{2,1,0:T(8,128)S(1)} %slice_add_fusion.cores_ref), custom_call_target="tpu_custom_call" | custom-call | tf_op jit(solution)/shard_map/pallas_call | solution.py:334
  193.6 22.3 %all_to_all.28.core_ref = bf16[8,80,512]{2,1,0:T(8,128)(2,1)S(1)} all-to-all(bf16[8,80,512]{2,1,0:T(8,128)(2,1)S(1)} %shard_map.66), channel_id=1, replica_groups=mesh['z'=8,'core'=2,'x'=4,'y'=8] {'z'}, dimensions={0} | all-to-all | bytes 1310720 | tf_op jit(solution)/shard_map/all_to_all | solution.py:347
  215.9 1.4 shard_map.67
  217.2 3.3 %collective-permute-start.22 = (bf16[8,64,128]{2,1,0:T(8,128)(2,1)S(1)}, bf16[8,64,128]{2,1,0:T(8,128)(2,1)S(1)}, u32[]{:S(2)}, u32[]{:S(2)}) collective-permute-start(bf16[8,64,128]{2,1,0:T(8,128)(2,1)S(1)} %get-tuple-element.13), channel_id=1, source_target_pairs={{0,32},{32,0},{1,33},{33,1},{2,34},{34,2},{3,35},{35,3},{4,36},{36... | collective-permute-start | bytes 393224 | tf_op jit(solution)/shard_map/ppermute | solution.py:392
  220.5 1.0 collective-permute-done.22
  (50 shorter events, 6.0 us)
Async XLA Ops:
  0.6 0.8 copy-start.2
  26.6 9.1 %collective-permute-start = (bf16[512,256]{1,0:T(8,128)(2,1)S(1)}, bf16[512,256]{1,0:T(8,128)(2,1)S(1)}, u32[]{:S(2)}, u32[]{:S(2)}) collective-permute-start(bf16[512,256]{1,0:T(8,128)(2,1)S(1)} %bitcast.57), channel_id=1, source_target_pairs={{0,8},{32,33},{1,9},{33,34},{2,10},{34,35},{3,11},{35,36},{4,12},{... | collective-permute-start | bytes 786440 | tf_op jit(solution)/shard_map/ppermute | solution.py:96
  29.8 7.9 %collective-permute-start.1 = (bf16[512,256]{1,0:T(8,128)(2,1)S(1)}, bf16[512,256]{1,0:T(8,128)(2,1)S(1)}, u32[]{:S(2)}, u32[]{:S(2)}) collective-permute-start(bf16[512,256]{1,0:T(8,128)(2,1)S(1)} %bitcast.58), channel_id=1, source_target_pairs={{0,24},{32,39},{1,25},{33,32},{2,26},{34,33},{3,27},{35,34},{4,28}... | collective-permute-start | bytes 786440 | tf_op jit(solution)/shard_map/ppermute | solution.py:96
  35.7 8.3 %collective-permute-start.2 = (bf16[512,256]{1,0:T(8,128)(2,1)S(1)}, bf16[512,256]{1,0:T(8,128)(2,1)S(1)}, u32[]{:S(2)}, u32[]{:S(2)}) collective-permute-start(bf16[512,256]{1,0:T(8,128)(2,1)S(1)} %collective-permute-done), channel_id=1, source_target_pairs={{0,8},{32,33},{1,9},{33,34},{2,10},{34,35},{3,11},{35,36},{4,12},{... | collective-permute-start | bytes 786440 | tf_op jit(solution)/shard_map/ppermute | solution.py:96
  37.7 12.2 %collective-permute-start.3 = (bf16[512,256]{1,0:T(8,128)(2,1)S(1)}, bf16[512,256]{1,0:T(8,128)(2,1)S(1)}, u32[]{:S(2)}, u32[]{:S(2)}) collective-permute-start(bf16[512,256]{1,0:T(8,128)(2,1)S(1)} %collective-permute-done.1), channel_id=1, source_target_pairs={{32,39},{33,32},{34,33},{35,34},{36,35},{37,36},{38,37},{39,38},{4... | collective-permute-start | bytes 786440 | tf_op jit(solution)/shard_map/ppermute | solution.py:96
  44.1 8.3 %collective-permute-start.4 = (bf16[512,256]{1,0:T(8,128)(2,1)S(1)}, bf16[512,256]{1,0:T(8,128)(2,1)S(1)}, u32[]{:S(2)}, u32[]{:S(2)}) collective-permute-start(bf16[512,256]{1,0:T(8,128)(2,1)S(1)} %collective-permute-done.2), channel_id=1, source_target_pairs={{32,33},{33,34},{34,35},{35,36},{36,37},{37,38},{38,39},{39,32},{4... | collective-permute-start | bytes 786440 | tf_op jit(solution)/shard_map/ppermute | solution.py:96
  46.8 17.8 %copy-start.3 = (bf16[2,512,256]{2,1,0:T(8,128)(2,1)S(1)}, bf16[2,512,256]{2,1,0:T(8,128)(2,1)}, u32[]{:S(2)}) copy-start(bf16[2,512,256]{2,1,0:T(8,128)(2,1)} %pad_maximum_fusion.low_ref.refs_0_) | copy-start | bytes 1572868
  46.9 26.6 %copy-start.4 = (bf16[2,512,256]{2,1,0:T(8,128)(2,1)}, bf16[2,512,256]{2,1,0:T(8,128)(2,1)S(1)}, u32[]{:S(2)}) copy-start(bf16[2,512,256]{2,1,0:T(8,128)(2,1)S(1)} %pad_maximum_fusion.1.low_ref.refs_1_) | copy-start | bytes 1572868
  46.9 31.3 %collective-permute-start.8 = (bf16[2,512,256]{2,1,0:T(8,128)(2,1)S(1)}, bf16[2,512,256]{2,1,0:T(8,128)(2,1)S(1)}, u32[]{:S(2)}, u32[]{:S(2)}) collective-permute-start(bf16[2,512,256]{2,1,0:T(8,128)(2,1)S(1)} %pad_maximum_fusion.1.low_ref.refs_1_), channel_id=1, source_target_pairs={{0,1},{32,40},{1,2},{33,41},{2,3},{34,42},{3,4},{35,43},{4,5},{36,... | collective-permute-start | bytes 1572872 | tf_op jit(solution)/shard_map/ppermute | solution.py:106
  53.2 44.6 %copy-start.11 = (s32[8,2]{0,1:T(2,128)S(1)}, s32[8,2]{0,1:T(2,128)}, u32[]{:S(2)}) copy-start(s32[8,2]{0,1:T(2,128)} %param.6) | copy-start | bytes 196
  55.2 25.6 %collective-permute-start.9 = (bf16[2,512,256]{2,1,0:T(8,128)(2,1)}, bf16[2,512,256]{2,1,0:T(8,128)(2,1)S(1)}, u32[]{:S(2)}, u32[]{:S(2)}) collective-permute-start(bf16[2,512,256]{2,1,0:T(8,128)(2,1)} %shard_map.60), channel_id=1, source_target_pairs={{0,7},{32,56},{1,0},{33,57},{2,1},{34,58},{3,2},{35,59},{4,3},{36,... | collective-permute-start | bytes 1572872 | tf_op jit(solution)/shard_map/ppermute | solution.py:106
  59.3 10.1 %collective-permute-start.5 = (bf16[512,256]{1,0:T(8,128)(2,1)S(1)}, bf16[512,256]{1,0:T(8,128)(2,1)S(1)}, u32[]{:S(2)}, u32[]{:S(2)}) collective-permute-start(bf16[512,256]{1,0:T(8,128)(2,1)S(1)} %collective-permute-done.3), channel_id=1, source_target_pairs={{32,39},{33,32},{34,33},{35,34},{36,35},{37,36},{38,37},{39,38},{4... | collective-permute-start | bytes 786440 | tf_op jit(solution)/shard_map/ppermute | solution.py:96
  61.3 11.3 %collective-permute-start.6 = (bf16[512,256]{1,0:T(8,128)(2,1)S(1)}, bf16[512,256]{1,0:T(8,128)(2,1)S(1)}, u32[]{:S(2)}, u32[]{:S(2)}) collective-permute-start(bf16[512,256]{1,0:T(8,128)(2,1)S(1)} %collective-permute-done.4), channel_id=1, source_target_pairs={{32,33},{33,34},{34,35},{35,36},{36,37},{37,38},{38,39},{39,32},{4... | collective-permute-start | bytes 786440 | tf_op jit(solution)/shard_map/ppermute | solution.py:96
  64.6 20.1 %collective-permute-start.7 = (bf16[2,512,256]{2,1,0:T(8,128)(2,1)S(1)}, bf16[2,512,256]{2,1,0:T(8,128)(2,1)S(1)}, u32[]{:S(2)}, u32[]{:S(2)}) collective-permute-start(bf16[2,512,256]{2,1,0:T(8,128)(2,1)S(1)} %copy-done.3), channel_id=1, source_target_pairs={{0,1},{32,40},{1,2},{33,41},{2,3},{34,42},{3,4},{35,43},{4,5},{36,... | collective-permute-start | bytes 1572872 | tf_op jit(solution)/shard_map/ppermute | solution.py:106
  75.5 11.2 %collective-permute-start.10 = (bf16[2,512,256]{2,1,0:T(8,128)(2,1)}, bf16[2,512,256]{2,1,0:T(8,128)(2,1)S(1)}, u32[]{:S(2)}, u32[]{:S(2)}) collective-permute-start(bf16[2,512,256]{2,1,0:T(8,128)(2,1)} %shard_map.61), channel_id=1, source_target_pairs={{0,7},{32,56},{1,0},{33,57},{2,1},{34,58},{3,2},{35,59},{4,3},{36,... | collective-permute-start | bytes 1572872 | tf_op jit(solution)/shard_map/ppermute | solution.py:106
  78.2 33.1 %copy-start.5 = (bf16[2,512,256]{2,1,0:T(8,128)(2,1)}, bf16[2,512,256]{2,1,0:T(8,128)(2,1)S(1)}, u32[]{:S(2)}) copy-start(bf16[2,512,256]{2,1,0:T(8,128)(2,1)S(1)} %collective-permute-done.8.refs_5_) | copy-start | bytes 1572868
  78.2 13.1 %collective-permute-start.12 = (bf16[2,512,256]{2,1,0:T(8,128)(2,1)S(1)}, bf16[2,512,256]{2,1,0:T(8,128)(2,1)S(1)}, u32[]{:S(2)}, u32[]{:S(2)}) collective-permute-start(bf16[2,512,256]{2,1,0:T(8,128)(2,1)S(1)} %collective-permute-done.8.refs_5_), channel_id=1, source_target_pairs={{0,1},{32,40},{1,2},{33,41},{2,3},{34,42},{3,4},{35,43},{4,5},{36,... | collective-permute-start | bytes 1572872 | tf_op jit(solution)/shard_map/ppermute | solution.py:106
  80.8 30.5 %copy-start.6 = (bf16[2,512,256]{2,1,0:T(8,128)(2,1)}, bf16[2,512,256]{2,1,0:T(8,128)(2,1)S(1)}, u32[]{:S(2)}) copy-start(bf16[2,512,256]{2,1,0:T(8,128)(2,1)S(1)} %collective-permute-done.9.refs_6_) | copy-start | bytes 1572868
  80.8 12.4 %collective-permute-start.13 = (bf16[2,512,256]{2,1,0:T(8,128)(2,1)S(1)}, bf16[2,512,256]{2,1,0:T(8,128)(2,1)}, u32[]{:S(2)}, u32[]{:S(2)}) collective-permute-start(bf16[2,512,256]{2,1,0:T(8,128)(2,1)S(1)} %collective-permute-done.9.refs_6_), channel_id=1, source_target_pairs={{0,7},{32,56},{1,0},{33,57},{2,1},{34,58},{3,2},{35,59},{4,3},{36,... | collective-permute-start | bytes 1572872 | tf_op jit(solution)/shard_map/ppermute | solution.py:106
  84.7 26.6 %copy-start.7 = (bf16[2,512,256]{2,1,0:T(8,128)(2,1)}, bf16[2,512,256]{2,1,0:T(8,128)(2,1)S(1)}, u32[]{:S(2)}) copy-start(bf16[2,512,256]{2,1,0:T(8,128)(2,1)S(1)} %collective-permute-done.7.refs_4_) | copy-start | bytes 1572868
  84.7 13.6 %collective-permute-start.11 = (bf16[2,512,256]{2,1,0:T(8,128)(2,1)S(1)}, bf16[2,512,256]{2,1,0:T(8,128)(2,1)S(1)}, u32[]{:S(2)}, u32[]{:S(2)}) collective-permute-start(bf16[2,512,256]{2,1,0:T(8,128)(2,1)S(1)} %collective-permute-done.7.refs_4_), channel_id=1, source_target_pairs={{0,1},{32,40},{1,2},{33,41},{2,3},{34,42},{3,4},{35,43},{4,5},{36,... | collective-permute-start | bytes 1572872 | tf_op jit(solution)/shard_map/ppermute | solution.py:106
  86.7 24.7 %copy-start.8 = (bf16[2,512,256]{2,1,0:T(8,128)(2,1)}, bf16[2,512,256]{2,1,0:T(8,128)(2,1)S(1)}, u32[]{:S(2)}) copy-start(bf16[2,512,256]{2,1,0:T(8,128)(2,1)S(1)} %collective-permute-done.10.refs_7_) | copy-start | bytes 1572868
  86.7 13.6 %collective-permute-start.14 = (bf16[2,512,256]{2,1,0:T(8,128)(2,1)S(1)}, bf16[2,512,256]{2,1,0:T(8,128)(2,1)}, u32[]{:S(2)}, u32[]{:S(2)}) collective-permute-start(bf16[2,512,256]{2,1,0:T(8,128)(2,1)S(1)} %collective-permute-done.10.refs_7_), channel_id=1, source_target_pairs={{0,7},{32,56},{1,0},{33,57},{2,1},{34,58},{3,2},{35,59},{4,3},{36,... | collective-permute-start | bytes 1572872 | tf_op jit(solution)/shard_map/ppermute | solution.py:106
  91.3 20.1 %copy-start.9 = (bf16[2,512,256]{2,1,0:T(8,128)(2,1)}, bf16[2,512,256]{2,1,0:T(8,128)(2,1)S(1)}, u32[]{:S(2)}) copy-start(bf16[2,512,256]{2,1,0:T(8,128)(2,1)S(1)} %collective-permute-done.12.refs_9_) | copy-start | bytes 1572868
  91.3 13.6 %collective-permute-start.16 = (bf16[2,512,256]{2,1,0:T(8,128)(2,1)S(1)}, bf16[2,512,256]{2,1,0:T(8,128)(2,1)}, u32[]{:S(2)}, u32[]{:S(2)}) collective-permute-start(bf16[2,512,256]{2,1,0:T(8,128)(2,1)S(1)} %collective-permute-done.12.refs_9_), channel_id=1, source_target_pairs={{0,1},{32,40},{1,2},{33,41},{2,3},{34,42},{3,4},{35,43},{4,5},{36,... | collective-permute-start | bytes 1572872 | tf_op jit(solution)/shard_map/ppermute | solution.py:106
  93.2 13.1 %collective-permute-start.17 = (bf16[2,512,256]{2,1,0:T(8,128)(2,1)}, bf16[2,512,256]{2,1,0:T(8,128)(2,1)}, u32[]{:S(2)}, u32[]{:S(2)}) collective-permute-start(bf16[2,512,256]{2,1,0:T(8,128)(2,1)} %collective-permute-done.13.refs_10_), channel_id=1, source_target_pairs={{0,7},{32,56},{1,0},{33,57},{2,1},{34,58},{3,2},{35,59},{4,3},{36,... | collective-permute-start | bytes 1572872 | tf_op jit(solution)/shard_map/ppermute | solution.py:106
  98.4 13.0 %copy-start.10 = (bf16[2,512,256]{2,1,0:T(8,128)(2,1)}, bf16[2,512,256]{2,1,0:T(8,128)(2,1)S(1)}, u32[]{:S(2)}) copy-start(bf16[2,512,256]{2,1,0:T(8,128)(2,1)S(1)} %collective-permute-done.11.refs_8_) | copy-start | bytes 1572868
  98.4 12.0 %collective-permute-start.15 = (bf16[2,512,256]{2,1,0:T(8,128)(2,1)S(1)}, bf16[2,512,256]{2,1,0:T(8,128)(2,1)}, u32[]{:S(2)}, u32[]{:S(2)}) collective-permute-start(bf16[2,512,256]{2,1,0:T(8,128)(2,1)S(1)} %collective-permute-done.11.refs_8_), channel_id=1, source_target_pairs={{0,1},{32,40},{1,2},{33,41},{2,3},{34,42},{3,4},{35,43},{4,5},{36,... | collective-permute-start | bytes 1572872 | tf_op jit(solution)/shard_map/ppermute | solution.py:106
  100.3 11.0 %collective-permute-start.18 = (bf16[2,512,256]{2,1,0:T(8,128)(2,1)}, bf16[2,512,256]{2,1,0:T(8,128)(2,1)}, u32[]{:S(2)}, u32[]{:S(2)}) collective-permute-start(bf16[2,512,256]{2,1,0:T(8,128)(2,1)} %collective-permute-done.14.refs_11_), channel_id=1, source_target_pairs={{0,7},{32,56},{1,0},{33,57},{2,1},{34,58},{3,2},{35,59},{4,3},{36,... | collective-permute-start | bytes 1572872 | tf_op jit(solution)/shard_map/ppermute | solution.py:106
  104.9 6.4 %collective-permute-start.20 = (bf16[2,512,256]{2,1,0:T(8,128)(2,1)}, bf16[2,512,256]{2,1,0:T(8,128)(2,1)}, u32[]{:S(2)}, u32[]{:S(2)}) collective-permute-start(bf16[2,512,256]{2,1,0:T(8,128)(2,1)} %collective-permute-done.16.refs_13_), channel_id=1, source_target_pairs={{0,1},{1,2},{2,3},{3,4},{4,5},{5,6},{6,7},{7,0},{8,9},{9,10},{10,1... | collective-permute-start | bytes 1572872 | tf_op jit(solution)/shard_map/ppermute | solution.py:106
  106.4 4.9 %collective-permute-start.19 = (bf16[2,512,256]{2,1,0:T(8,128)(2,1)}, bf16[2,512,256]{2,1,0:T(8,128)(2,1)}, u32[]{:S(2)}, u32[]{:S(2)}) collective-permute-start(bf16[2,512,256]{2,1,0:T(8,128)(2,1)} %collective-permute-done.17.refs_14_), channel_id=1, source_target_pairs={{0,7},{1,0},{2,1},{3,2},{4,3},{5,4},{6,5},{7,6},{8,15},{9,8},{10,9... | collective-permute-start | bytes 1572872 | tf_op jit(solution)/shard_map/ppermute | solution.py:106
  116.8 1.4 copy-start
  118.1 18.5 %all-to-all-start.1 = ((bf16[8,64,512]{2,1,0:T(8,128)(2,1)}), bf16[8,64,512]{2,1,0:T(8,128)(2,1)S(1)}, u32[]{:S(2)}, u32[]{:S(2)}) async-start(bf16[8,64,512]{2,1,0:T(8,128)(2,1)} %get-tuple-element.8), calls=%async_computation.1 | async-start | bytes 1048576 | tf_op jit(solution)/shard_map/all_to_all | solution.py:347
  155.2 7.1 %collective-permute-start.21 = (bf16[8,64,256]{2,1,0:T(8,128)(2,1)S(1)}, bf16[8,64,256]{2,1,0:T(8,128)(2,1)S(1)}, u32[]{:S(2)}, u32[]{:S(2)}) collective-permute-start(bf16[8,64,256]{2,1,0:T(8,128)(2,1)S(1)} %shard_map.64.own_ref), channel_id=1, source_target_pairs={{0,32},{32,0},{1,33},{33,1},{2,34},{34,2},{3,35},{35,3},{4,36},{36... | collective-permute-start | bytes 786440 | tf_op jit(solution)/shard_map/ppermute | solution.py:377
  163.7 52.2 %copy-start.1 = (bf16[8,512,256]{2,1,0:T(8,128)(2,1)S(1)}, bf16[8,512,256]{2,1,0:T(8,128)(2,1)}, u32[]{:S(2)}) copy-start(bf16[8,512,256]{2,1,0:T(8,128)(2,1)} %copy-done) | copy-start | bytes 6291460
  217.2 4.2 %collective-permute-start.22 = (bf16[8,64,128]{2,1,0:T(8,128)(2,1)S(1)}, bf16[8,64,128]{2,1,0:T(8,128)(2,1)S(1)}, u32[]{:S(2)}, u32[]{:S(2)}) collective-permute-start(bf16[8,64,128]{2,1,0:T(8,128)(2,1)S(1)} %get-tuple-element.13), channel_id=1, source_target_pairs={{0,32},{32,0},{1,33},{33,1},{2,34},{34,2},{3,35},{35,3},{4,36},{36... | collective-permute-start | bytes 393224 | tf_op jit(solution)/shard_map/ppermute | solution.py:392
